TPU v7x, 512 devices: a whole 4x4x16 slice. The times are simulated.
512 devices in a mesh: seg: 64 (over z, x), sub: 8 (over y, core).
Axes of the slice: x: 4, y: 4, z: 16, core: 2. Of those that a mesh axis runs over, the one named last changes fastest.
Arguments:
- near_blocks: bfloat16 [1024, 10, 256, 256], P(('seg', 'sub')), may hold values from -0.375 to 0.375
- sample_cols: bfloat16 [262144, 256], P(('seg', 'sub')), may hold values from -6 to 6
- near_list: int32 [1024, 10], P(('seg', 'sub')), may hold values from -1 to 1023, as said below
- row_basis_t: bfloat16 [1024, 64, 256], P(('seg', 'sub')), may hold values from -0.75 to 0.75
- col_basis_t: bfloat16 [1024, 64, 256], P(('seg', 'sub')), may hold values from -0.375 to 0.375
- couplings: bfloat16 [64, 8, 64, 64, 128], P('seg', 'sub'), may hold values from -0.125 to 0.125
- far_source: int32 [64, 8, 64, 2], P('seg', 'sub'), may hold values from 0 to 2
- far_dest: int32 [64, 8, 64, 2], P('seg', 'sub'), may hold values from 0 to 1
Outputs:
- samples: bfloat16 [262144, 256], P(('seg', 'sub'))
- segment_factor: float32 [16384, 256], P('seg')
- transfers: bfloat16 [64, 3, 256, 256], P('seg')
Inputs may be any that keep to these rules, and one draw needn't show every extreme that they name: `near_list`: entry 0 of every list is the leaf itself; -1 marks padding and stands only after the real entries; every other entry names a leaf held by the same device or by the device just before or just after it in the order of seg, then sub. `far_source`: entry [s', u, s, c] is the local leaf of device (s', u) whose far projection fills slot c toward device (s, u); the value 2 marks an empty slot. `far_dest`: entry [s, u, s', c] is the local leaf of device (s, u) that slot c from device (s', u) serves.
All inputs are finite; a program needn't handle non-finite values.
Results may differ from a plain program's by a relative error of at most 0.013.
Values may be sent and summed in bfloat16 or wider, within the bound.
A program may use at most 64 MiB of HBM per device.

v0:
```python
import jax
import jax.numpy as jnp
from jax import lax
from jax.sharding import PartitionSpec as P

LEVELS = 3


def padded(value, sides, width):
    for axis, dim in sides:
        size, length = (lax.axis_size(axis), value.shape[dim])
        up = [(i, (i + 1) % size) for i in range(size - 1)]
        down = [(j, i) for i, j in up]
        last = lax.slice_in_dim(value, length - width, length, axis=dim)
        leading = lax.slice_in_dim(value, 0, width, axis=dim)
        before = lax.ppermute(last, axis, up)
        after = lax.ppermute(leading, axis, down)
        value = jnp.concatenate([before, value, after], axis=dim)
    return value


def from_partner(value, axis, distance):
    mask = 2**distance
    pairs = [(source, source ^ mask) for source in range(lax.axis_size(axis))]
    return lax.ppermute(value, axis, pairs)


def body(
    near_blocks, sample_cols, near_list, row_basis_t, col_basis_t, couplings, far_source, far_dest
):
    leaf_count, near_count, leaf_rows, _ = near_blocks.shape
    sample_width = sample_cols.shape[1]
    rank_width = row_basis_t.shape[1]
    seg_count = lax.axis_size("seg")
    slot_number_count = far_source.shape[3]
    random_cols = sample_cols.reshape(leaf_count, leaf_rows, sample_width)
    basis_projector = jnp.einsum(
        "jra,jas->jrs", col_basis_t, random_cols, preferred_element_type=jnp.float32
    ).astype(jnp.bfloat16)
    extended = padded(sample_cols, ((("seg", "sub"), 0),), leaf_count * leaf_rows)
    extended = extended.reshape(3 * leaf_count, leaf_rows, sample_width)
    base_leaf = (lax.axis_index(("seg", "sub")) - 1) * leaf_count
    usable = near_list >= 0
    position = jnp.where(usable, near_list - base_leaf, 0)
    chosen = extended[position]
    chosen = jnp.where(usable[:, :, None, None], chosen, jnp.zeros_like(chosen))
    near_part = jnp.einsum(
        "lkab,lkbs->las", near_blocks, chosen, preferred_element_type=jnp.float32
    )
    leaf_range = jnp.arange(leaf_count, dtype=jnp.int32)
    routing = far_dest[0, 0][:, :, None] == leaf_range[None, None, :]
    coupling_set = jnp.transpose(
        couplings[0, 0].reshape(seg_count, rank_width, slot_number_count, rank_width), (1, 0, 2, 3)
    )
    masked = jnp.where(
        jnp.transpose(routing, (2, 0, 1))[:, None, :, :, None],
        coupling_set[None],
        jnp.zeros((), jnp.bfloat16),
    )
    masked = masked.reshape(leaf_count * rank_width, seg_count * slot_number_count * rank_width)
    selection_choice = (far_source[0, 0][:, :, None] == leaf_range[None, None, :]).astype(
        jnp.bfloat16
    )
    outgoing = jnp.einsum(
        "zgy,ykf->zgkf", selection_choice, basis_projector, preferred_element_type=jnp.float32
    ).astype(jnp.bfloat16)
    incoming = lax.all_to_all(outgoing, "seg", split_axis=0, concat_axis=0, tiled=True)
    far_total = jnp.dot(
        masked,
        incoming.reshape(seg_count * slot_number_count * rank_width, sample_width),
        preferred_element_type=jnp.float32,
    )
    far_coeff = far_total.astype(jnp.bfloat16).reshape(leaf_count, rank_width, sample_width)
    distant_portion = jnp.einsum(
        "lra,lrs->las", row_basis_t, far_coeff, preferred_element_type=jnp.float32
    )
    samples = (
        (near_part + distant_portion)
        .astype(jnp.bfloat16)
        .reshape(leaf_count * leaf_rows, sample_width)
    )
    gram_local = lax.dot_general(
        samples, samples, (((0,), (0,)), ((), ())), preferred_element_type=jnp.float32
    )
    row_total = lax.axis_size("sub") * leaf_count * leaf_rows
    current = lax.psum(gram_local.astype(jnp.bfloat16), "sub").astype(jnp.float32) / row_total
    gram_levels = [current]
    for segment_position_index in range(LEVELS):
        partner = from_partner(current.astype(jnp.bfloat16), "seg", segment_position_index).astype(
            current.dtype
        )
        current = (current + partner) * 0.5
        gram_levels.append(current)
    stacked = jnp.stack(gram_levels)
    triangles = jnp.linalg.cholesky(stacked)
    segment_factor = jnp.swapaxes(triangles[0], 0, 1)
    solved = jax.vmap(
        lambda upper_one, lower_one: jax.scipy.linalg.solve_triangular(
            upper_one, lower_one, lower=True
        )
    )(triangles[1:], triangles[:-1])
    transfers = jnp.swapaxes(solved, 1, 2).astype(jnp.bfloat16)[None]
    return (samples, segment_factor, transfers)


def solution(mesh):
    in_specs = (
        P(("seg", "sub"), None, None, None),
        P(("seg", "sub"), None),
        P(("seg", "sub"), None),
        P(("seg", "sub"), None, None),
        P(("seg", "sub"), None, None),
        P("seg", "sub", None, None, None),
        P("seg", "sub", None, None),
        P("seg", "sub", None, None),
    )
    out_specs = (P(("seg", "sub"), None), P("seg", None), P("seg", None, None, None))
    return jax.shard_map(body, mesh=mesh, in_specs=in_specs, out_specs=out_specs, check_vma=False)
```

profile of v0, /device:TPU:1, one launch (start us, length us, event | category | flops | bytes accessed | tf_op | source)
XLA Modules:
  0.0 555.6 jit_solution(11103013563132528204)
XLA Ops:
  7.2 1.3 convolution_convert_fusion.3
  8.5 2.0 convolution_convert_fusion
  10.5 4.4 copy.66
  14.9 19.5 %all-to-all-start = ((bf16[64,2,64,256]{3,2,1,0:T(8,128)(2,1)}), bf16[64,2,64,256]{3,2,1,0:T(8,128)(2,1)}, u32[]{:S(2)}, u32[]{:S(2)}) async-start(bf16[64,2,64,256]{3,2,1,0:T(8,128)(2,1)} %copy.66), calls=%async_computation | async-start | bytes 8388608 | tf_op jit(solution)/shard_map/all_to_all | solution.py:67
  34.4 4.0 collective-permute-start
  38.5 1.9 collective-permute-start.1
  40.5 5.3 reshape_squeeze.3
  45.9 4.0 copy.95
  49.9 2.3 broadcast_select_fusion
  52.2 12.6 %copy.64 = bf16[2,64,64,2,64]{4,3,2,1,0:T(2,128)(2,1)} copy(bf16[2,64,64,2,64]{4,2,3,1,0:T(8,128)(2,1)} %broadcast_select_fusion) | data formatting | bytes 4194304 | tf_op jit(solution)/shard_map/jit(_where)/select_n | solution.py:55
  64.8 21.4 %select_n.33 = bf16[128,8192]{1,0:T(8,128)(2,1)} reshape(bf16[2,64,64,2,64]{4,3,2,1,0:T(2,128)(2,1)} %copy.64) | data formatting | bytes 4194304 | tf_op jit(solution)/shard_map/jit(_where)/select_n | solution.py:55
  87.0 1.2 pad_maximum_fusion.1
  88.1 2.4 gather_fusion
  90.6 2.6 fusion.4
  93.2 124.8 %all-to-all-done = bf16[64,2,64,256]{3,2,1,0:T(8,128)(2,1)} async-done(((bf16[64,2,64,256]{3,2,1,0:T(8,128)(2,1)}), bf16[64,2,64,256]{3,2,1,0:T(8,128)(2,1)}, u32[]{:S(2)}, u32[]{:S(2)}) %all-to-all-start) | async-done | bytes 4194336 | tf_op jit(solution)/shard_map/all_to_all | solution.py:67
  218.0 3.6 convolution_convert_fusion.2
  222.6 0.9 fusion.8
  223.5 81.2 %all-reduce.3.cloned.1.call-done = bf16[256,256]{0,1:T(8,128)(2,1)} async-done(((bf16[256,256]{0,1:T(8,128)(2,1)}), bf16[256,256]{0,1:T(8,128)(2,1)}) %all-reduce.3.cloned.1.call-update) | async-done | bytes 131088 | tf_op jit(solution)/shard_map/psum | solution.py:86
  304.7 0.9 fusion.16
  305.7 2.3 collective-permute-start.2
  308.0 3.4 collective-permute-done.2
  311.4 1.0 fusion.17
  312.3 3.8 collective-permute-start.3
  316.8 2.8 collective-permute-done.3
  319.6 1.0 fusion.29
  320.6 2.4 collective-permute-start.4
  324.2 2.2 collective-permute-done.4
  326.4 1.1 fusion.20
  328.2 1.1 pad_maximum_fusion
  329.3 2.5 copy.69
  331.9 1.4 fusion.9
  333.3 1.0 copy-done.2
  334.3 46.9 %custom-call.17 = f32[4,128,128]{2,1,0:T(8,128)S(1)} custom-call(f32[4,128,128]{2,1,0:T(8,128)S(1)} %cholesky.122), custom_call_target="Cholesky" | custom-call | tf_op jit(solution)/shard_map/jit(cholesky)/cholesky | solution.py:95
  381.2 1.1 cholesky.117
  382.3 39.3 %custom-call.18 = f32[4,1,128,128]{2,3,1,0:T(8,128)S(1)} custom-call(f32[4,1,128,128]{3,2,1,0:T(8,128)S(1)} %select_bitcast_fusion), custom_call_target="InvertDiagBlocksLowerTriangular" | custom-call | tf_op jit(solution)/shard_map/jit(cholesky)/cholesky | solution.py:95
  421.6 2.1 constant_dynamic-update-slice_fusion.1
  423.7 1.6 convolution_subtract_fusion.1
  425.4 46.9 %custom-call.19 = f32[4,128,128]{2,1,0:T(8,128)S(1)} custom-call(f32[4,128,128]{2,1,0:T(8,128)S(1)} %convolution_subtract_fusion.1), custom_call_target="Cholesky" | custom-call | tf_op jit(solution)/shard_map/jit(cholesky)/cholesky | solution.py:95
  473.2 1.4 select_select_fusion
  474.7 0.9 copy-done.1
  476.4 5.4 while.1
  477.0 2.1 bitcast_dynamic-update-slice_fusion.2
  479.7 2.1 bitcast_dynamic-update-slice_fusion.2
  481.7 60.4 %custom-call.20 = f32[3,2,128,128]{2,3,1,0:T(8,128)} custom-call(f32[3,2,128,128]{3,2,1,0:T(8,128)} %bitcast.101), custom_call_target="InvertDiagBlocksLowerTriangular" | custom-call | tf_op jit(solution)/shard_map/vmap(jit(_solve_triangular))/triangular_solve | solution.py:98
  542.1 1.7 fusion.31
  543.8 1.5 convolution_subtract_fusion
  545.9 0.9 copy.76
  546.8 1.8 copy.75
  (57 shorter events, 8.0 us)
Async XLA Ops:
  7.2 83.4 %copy-start = (bf16[2,10,256,256]{3,2,1,0:T(8,128)(2,1)S(1)}, bf16[2,10,256,256]{3,2,1,0:T(8,128)(2,1)}, u32[]{:S(2)}) copy-start(bf16[2,10,256,256]{3,2,1,0:T(8,128)(2,1)} %param.8) | copy-start | bytes 7864324
  14.9 19.6 %copy-start.4 = (bf16[512,256]{1,0:T(8,128)(2,1)S(1)}, bf16[512,256]{1,0:T(8,128)(2,1)}, u32[]{:S(2)}) copy-start(bf16[512,256]{1,0:T(8,128)(2,1)} %param.9) | copy-start | bytes 786436
  14.9 25.6 %copy-start.13 = (s32[2,10]{1,0:T(2,128)S(1)}, s32[2,10]{1,0:T(2,128)}, u32[]{:S(2)}) copy-start(s32[2,10]{1,0:T(2,128)} %param.10) | copy-start | bytes 244
  14.9 203.1 %all-to-all-start = ((bf16[64,2,64,256]{3,2,1,0:T(8,128)(2,1)}), bf16[64,2,64,256]{3,2,1,0:T(8,128)(2,1)}, u32[]{:S(2)}, u32[]{:S(2)}) async-start(bf16[64,2,64,256]{3,2,1,0:T(8,128)(2,1)} %copy.66), calls=%async_computation | async-start | bytes 8388608 | tf_op jit(solution)/shard_map/all_to_all | solution.py:67
  34.4 270.3 %all-reduce.3.cloned.1.call-start = ((), (), s32[]{:S(2)}) async-start(), calls=%async_computation.1 | async-start | bytes 262144 | tf_op jit(solution)/shard_map/psum | solution.py:86
  34.4 51.8 %collective-permute-start = (bf16[512,256]{1,0:T(8,128)(2,1)S(1)}, bf16[512,256]{1,0:T(8,128)(2,1)S(1)}, u32[]{:S(2)}, u32[]{:S(2)}) collective-permute-start(bf16[512,256]{1,0:T(8,128)(2,1)S(1)} %copy-done.4), channel_id=1, source_target_pairs={{0,1},{1,2},{2,3},{3,4},{4,5},{5,6},{6,7},{7,8},{8,9},{9,10},{10,1... | collective-permute-start | bytes 786440 | tf_op jit(solution)/shard_map/ppermute | solution.py:16
  38.5 48.5 %collective-permute-start.1 = (bf16[512,256]{1,0:T(8,128)(2,1)S(1)}, bf16[512,256]{1,0:T(8,128)(2,1)}, u32[]{:S(2)}, u32[]{:S(2)}) collective-permute-start(bf16[512,256]{1,0:T(8,128)(2,1)S(1)} %copy-done.4), channel_id=1, source_target_pairs={{1,0},{2,1},{3,2},{4,3},{5,4},{6,5},{7,6},{8,7},{9,8},{10,9},{11,1... | collective-permute-start | bytes 786440 | tf_op jit(solution)/shard_map/ppermute | solution.py:17
  45.9 4.0 copy-start.12
  86.3 0.7 copy-start.9
  218.0 3.6 copy-start.10
  221.9 0.7 copy-start.8
  305.7 5.7 %collective-permute-start.2 = (bf16[256,256]{0,1:T(8,128)(2,1)S(1)}, bf16[256,256]{0,1:T(8,128)(2,1)S(1)}, u32[]{:S(2)}, u32[]{:S(2)}) collective-permute-start(bf16[256,256]{0,1:T(8,128)(2,1)S(1)} %fusion.16), channel_id=1, source_target_pairs={{0,8},{8,0},{16,24},{24,16},{32,40},{40,32},{48,56},{56,48},{64,72... | collective-permute-start | bytes 393224 | tf_op jit(solution)/shard_map/ppermute | solution.py:25
  312.3 7.2 %collective-permute-start.3 = (bf16[256,256]{0,1:T(8,128)(2,1)S(1)}, bf16[256,256]{0,1:T(8,128)(2,1)S(1)}, u32[]{:S(2)}, u32[]{:S(2)}) collective-permute-start(bf16[256,256]{0,1:T(8,128)(2,1)S(1)} %get-tuple-element.44), channel_id=1, source_target_pairs={{0,16},{8,24},{16,0},{24,8},{32,48},{40,56},{48,32},{56,40},{64,80... | collective-permute-start | bytes 393224 | tf_op jit(solution)/shard_map/ppermute | solution.py:25
  319.5 4.6 copy-start.6
  320.6 5.8 %collective-permute-start.4 = (bf16[256,256]{0,1:T(8,128)(2,1)S(1)}, bf16[256,256]{0,1:T(8,128)(2,1)}, u32[]{:S(2)}, u32[]{:S(2)}) collective-permute-start(bf16[256,256]{0,1:T(8,128)(2,1)S(1)} %get-tuple-element.39), channel_id=1, source_target_pairs={{0,32},{8,40},{16,48},{24,56},{32,0},{40,8},{48,16},{56,24},{64,96... | collective-permute-start | bytes 393224 | tf_op jit(solution)/shard_map/ppermute | solution.py:25
  327.5 0.7 copy-start.3
  331.9 50.4 %copy-start.11 = (pred[128,128]{1,0:T(8,128)(4,1)S(1)}, pred[128,128]{1,0:T(8,128)(4,1)}, u32[]{:S(2)}) copy-start(pred[128,128]{1,0:T(8,128)(4,1)} %iota_compare_fusion.1) | copy-start | bytes 49156
  333.3 1.0 copy-start.2
  334.3 138.9 %copy-start.5 = (pred[256,256]{1,0:T(8,128)(4,1)S(1)}, pred[256,256]{1,0:T(8,128)(4,1)}, u32[]{:S(2)}) copy-start(pred[256,256]{1,0:T(8,128)(4,1)} %iota_compare_fusion) | copy-start | bytes 196612
  425.4 51.0 %copy-start.14 = (s32[2]{0:T(128)S(1)}, s32[2]{0:T(128)}, u32[]{:S(2)}) copy-start(s32[2]{0:T(128)} %iota_multiply_fusion) | copy-start | bytes 28
  474.6 1.0 copy-start.1
  542.1 3.2 copy-start.7
Sparse Core Ops, SparseCore 0:
  223.6 81.0 all-reduce.2
where the time goes:
time: 566 us; the launch traced here: 556 us
  waiting for transfers between devices  214 us (38%)
  other arithmetic  208 us (37%)
  local copies, waits for them, and re-layouts  66.8 us (12%)
  starting transfers between devices  34 us (6%)
  matrix products  18.1 us (3%)
  between operations  14.6 us (3%)
    another operation x9, other arithmetic, body(): triangles = jnp.linalg.cholesky(stacked)  135 us
    all_to_all x1, waiting for transfers between devices, body(): lax.all_to_all(outgoing, 'seg', split_axis=0, concat_axis=0, tiled=True)  125 us
    psum x1, waiting for transfers between devices, body(): lax.psum(gram_local.astype(jnp.bfloat16), 'sub').astype(jnp.float32)  81.2 us
    another operation x3, other arithmetic, body(): jax.scipy.linalg.solve_triangular(upper_one, lower_one, lower=True)  61 us
    select_n x2, local copies, waits for them, and re-layouts, body(): jnp.where(jnp.transpose(routing, (2, 0, 1))[:, None, :, :, None], couplin...  34 us
    all_to_all x1, starting transfers between devices, body(): lax.all_to_all(outgoing, 'seg', split_axis=0, concat_axis=0, tiled=True)  19.5 us
  transfers between devices with their start and end apart: 7, of which 5 were waited for; matrix products, arithmetic and copies ran while one was open for 10% of the time, Pallas kernels for 0%

commit v1 on v0

v1 whole, which is shorter than its diff:
```python
import jax
import jax.numpy as jnp
from jax import lax
from jax.experimental import pallas as pl
from jax.experimental.pallas import tpu as pltpu
from jax.sharding import PartitionSpec as P

LEVELS = 3

BLOCK = 32
GROUP = 8


def dot32(a, b, dims):
    return lax.dot_general(
        a, b, (dims, ((), ())), precision=lax.Precision.HIGHEST, preferred_element_type=jnp.float32
    )


def eliminate(blocks):
    size = blocks[0].shape[0]
    rows = lax.broadcasted_iota(jnp.int32, (size, size), 0)
    cols = lax.broadcasted_iota(jnp.int32, (size, size), 1)
    eye = (rows == cols).astype(jnp.float32)
    sub = lax.broadcasted_iota(jnp.int32, (GROUP, 1), 0)
    states = []
    for d in blocks:
        x = jnp.concatenate([d, eye], axis=1)
        states.append([x[g * GROUP : (g + 1) * GROUP] for g in range(size // GROUP)])
    for k in range(size):
        own, r = divmod(k, GROUP)
        for x in states:
            line = x[own][r : r + 1, :]
            scale = lax.rsqrt(line[:, k : k + 1])
            line = line * scale
            for g in range(own, size // GROUP):
                factor = x[g][:, k : k + 1] * scale
                if g == own:
                    below = x[g] - jnp.where(sub > r, factor, 0.0) * line
                    x[g] = jnp.where(sub == r, line, below)
                else:
                    x[g] = x[g] - factor * line
    out = []
    for x in states:
        x = jnp.concatenate(x, axis=0)
        out.append((jnp.where(rows <= cols, x[:, :size], 0.0), x[:, size:]))
    return out


def factor_kernel(gram_ref, factor_ref, transfer_ref, work, upper):
    count, n, _ = work.shape
    lanes = lax.broadcasted_iota(jnp.int32, (1, n), 1)
    work[...] = gram_ref[...]
    upper[...] = jnp.zeros_like(upper)
    for at in range(0, n, BLOCK):
        end = at + BLOCK
        inside = (lanes >= at) & (lanes < end)
        pairs = eliminate([work[i, at:end, at:end] for i in range(count)])
        for i in range(count):
            r_block, v_block = pairs[i]
            panel = dot32(v_block, work[i, at:end, :], ((1,), (0,)))
            upper[i, at:end, :] = jnp.where(lanes >= end, panel, 0.0)
            upper[i, at:end, at:end] = r_block
            work[i, at:end, :] = jnp.where(lanes < at, panel, 0.0)
            work[i, at:end, at:end] = v_block
            if end < n:
                step = jnp.where(lanes < at, panel, upper[i, at:end, :])
                step = jnp.where(inside, work[i, at:end, :], step)
                rest = jnp.where(inside, 0.0, work[i, end:, :])
                work[i, end:, :] = rest - dot32(panel[:, end:], step, ((0,), (0,)))
    factor_ref[...] = upper[0]
    for i in range(1, count):
        transfer_ref[i - 1] = dot32(upper[i - 1], work[i], ((1,), (1,))).astype(jnp.bfloat16)


def factors(stacked):
    count, n, _ = stacked.shape
    return pl.pallas_call(
        factor_kernel,
        out_shape=(
            jax.ShapeDtypeStruct((n, n), jnp.float32),
            jax.ShapeDtypeStruct((count - 1, n, n), jnp.bfloat16),
        ),
        in_specs=[pl.BlockSpec(memory_space=pltpu.VMEM)],
        out_specs=[pl.BlockSpec(memory_space=pltpu.VMEM)] * 2,
        scratch_shapes=[
            pltpu.VMEM((count, n, n), jnp.float32),
            pltpu.VMEM((count, n, n), jnp.float32),
        ],
    )(stacked)


FAR_UNROLL = 4


def far_kernel(
    source_ref, dest_ref, gathered_ref, coupling_ref, basis_ref, near_ref, samples_ref, gram_ref
):
    leaf_count, rank, leaf_rows = basis_ref.shape
    seg_count = coupling_ref.shape[0]
    slots = coupling_ref.shape[2] // rank
    width = gathered_ref.shape[2]
    lane = lax.broadcasted_iota(jnp.int32, (1, slots * rank), 1) // rank

    def step(index, total):
        left, right = [], []
        for part in range(FAR_UNROLL):
            seg = index * FAR_UNROLL + part
            key = jnp.full((1, slots * rank), -1, jnp.int32)
            for slot in range(slots):
                source = source_ref[seg * slots + slot]
                served = jnp.where(source < leaf_count, dest_ref[seg * slots + slot], -1)
                key = jnp.where(lane == slot, served, key)
                start = pl.multiple_of(jnp.minimum(source, leaf_count - 1) * rank, rank)
                right.append(gathered_ref[seg, pl.ds(start, rank), :])
            block = coupling_ref[seg]
            left.append(
                jnp.concatenate(
                    [jnp.where(key == leaf, block, jnp.zeros_like(block)) for leaf in range(leaf_count)],
                    axis=0,
                )
            )
        return total + jnp.dot(
            jnp.concatenate(left, axis=1),
            jnp.concatenate(right, axis=0),
            preferred_element_type=jnp.float32,
        )

    total = lax.fori_loop(
        0, seg_count // FAR_UNROLL, step, jnp.zeros((leaf_count * rank, width), jnp.float32)
    )
    coeff = total.astype(jnp.bfloat16)
    for leaf in range(leaf_count):
        rows = slice(leaf * leaf_rows, (leaf + 1) * leaf_rows)
        far = lax.dot_general(
            basis_ref[leaf],
            coeff[leaf * rank : (leaf + 1) * rank],
            (((0,), (0,)), ((), ())),
            preferred_element_type=jnp.float32,
        )
        samples_ref[rows, :] = (near_ref[rows, :] + far).astype(jnp.bfloat16)
    samples = samples_ref[...]
    gram_ref[...] = lax.dot_general(
        samples, samples, (((0,), (0,)), ((), ())), preferred_element_type=jnp.float32
    ).astype(gram_ref.dtype)


def far_and_gram(source, dest, gathered, coupling, basis, near):
    rows, width = near.shape
    smem, vmem = pl.BlockSpec(memory_space=pltpu.SMEM), pl.BlockSpec(memory_space=pltpu.VMEM)
    return pl.pallas_call(
        far_kernel,
        out_shape=(
            jax.ShapeDtypeStruct((rows, width), jnp.bfloat16),
            jax.ShapeDtypeStruct((width, width), jnp.bfloat16),
        ),
        in_specs=[smem, smem, vmem, vmem, vmem, vmem],
        out_specs=[vmem, vmem],
        compiler_params=pltpu.CompilerParams(vmem_limit_bytes=32 * 2**20),
    )(source, dest, gathered, coupling, basis, near)


def padded(value, sides, width):
    for axis, dim in sides:
        size, length = (lax.axis_size(axis), value.shape[dim])
        up = [(i, (i + 1) % size) for i in range(size - 1)]
        down = [(j, i) for i, j in up]
        last = lax.slice_in_dim(value, length - width, length, axis=dim)
        leading = lax.slice_in_dim(value, 0, width, axis=dim)
        before = lax.ppermute(last, axis, up)
        after = lax.ppermute(leading, axis, down)
        value = jnp.concatenate([before, value, after], axis=dim)
    return value


def from_partner(value, axis, distance):
    mask = 2**distance
    pairs = [(source, source ^ mask) for source in range(lax.axis_size(axis))]
    return lax.ppermute(value, axis, pairs)


def paired_sum(value, axis, distance):
    partner = from_partner(value, axis, distance)
    return value.astype(jnp.float32) + partner.astype(jnp.float32)


def body(
    near_blocks, sample_cols, near_list, row_basis_t, col_basis_t, couplings, far_source, far_dest
):
    leaf_count, near_count, leaf_rows, _ = near_blocks.shape
    sample_width = sample_cols.shape[1]
    rank_width = row_basis_t.shape[1]
    seg_count = lax.axis_size("seg")
    slot_number_count = far_source.shape[3]
    random_cols = sample_cols.reshape(leaf_count, leaf_rows, sample_width)
    basis_projector = jnp.einsum(
        "jra,jas->jrs", col_basis_t, random_cols, preferred_element_type=jnp.float32
    ).astype(jnp.bfloat16)
    source_rows = jnp.swapaxes(far_source[0, 0], 0, 1).astype(jnp.bfloat16)
    source_rows = jnp.pad(
        source_rows, ((0, 16 - slot_number_count), (0, sample_width - seg_count))
    )
    packed = jnp.concatenate(
        [basis_projector.reshape(leaf_count * rank_width, sample_width), source_rows], axis=0
    )
    gathered = lax.all_gather(packed, "seg")
    sources = gathered[:, leaf_count * rank_width : leaf_count * rank_width + slot_number_count, :]
    sources = lax.dynamic_slice_in_dim(sources, lax.axis_index("seg"), 1, axis=2)
    sources = sources.astype(jnp.int32).reshape(seg_count * slot_number_count)
    extended = padded(sample_cols, ((("seg", "sub"), 0),), leaf_count * leaf_rows)
    extended = extended.reshape(3 * leaf_count, leaf_rows, sample_width)
    base_leaf = (lax.axis_index(("seg", "sub")) - 1) * leaf_count
    usable = near_list >= 0
    position = jnp.where(usable, near_list - base_leaf, 0)
    chosen = extended[position]
    chosen = jnp.where(usable[:, :, None, None], chosen, jnp.zeros_like(chosen))
    near_part = jnp.einsum(
        "lkab,lkbs->las", near_blocks, chosen, preferred_element_type=jnp.float32
    )
    samples, gram_local = far_and_gram(
        sources,
        far_dest.reshape(seg_count * slot_number_count),
        gathered,
        couplings[0, 0],
        row_basis_t,
        near_part.reshape(leaf_count * leaf_rows, sample_width),
    )
    row_total = lax.axis_size("sub") * leaf_count * leaf_rows
    current = gram_local
    for distance in range((lax.axis_size("sub") - 1).bit_length()):
        total = paired_sum(current, "sub", distance)
        current = total.astype(jnp.bfloat16)
    gram_levels = [total / row_total]
    for distance in range(LEVELS):
        total = paired_sum(gram_levels[-1].astype(jnp.bfloat16), "seg", distance) * 0.5
        gram_levels.append(total)
    segment_factor, transfers = factors(jnp.stack(gram_levels))
    return (samples, segment_factor, transfers[None])


def solution(mesh):
    in_specs = (
        P(("seg", "sub"), None, None, None),
        P(("seg", "sub"), None),
        P(("seg", "sub"), None),
        P(("seg", "sub"), None, None),
        P(("seg", "sub"), None, None),
        P("seg", "sub", None, None, None),
        P("seg", "sub", None, None),
        P("seg", "sub", None, None),
    )
    out_specs = (P(("seg", "sub"), None), P("seg", None), P("seg", None, None, None))
    return jax.shard_map(body, mesh=mesh, in_specs=in_specs, out_specs=out_specs, check_vma=False)
```

time: 566 us -> 257 us (0.45)
  other arithmetic: 208 us -> 6.55 us
  waiting for transfers between devices: 214 us -> 144 us
  local copies, waits for them, and re-layouts: 66.8 us -> 8.79 us
  Pallas kernels: 0 us -> 37.5 us
  matrix products: 18.1 us -> 3.83 us
    another operation x16 -> x5, other arithmetic: 200 us -> 1.23 us  [body(): segment_factor, transfers = factors(jnp.stack(gram_levels))]
    all_gather x0 -> x1, waiting for transfers between devices: none -> 126 us  [body(): gathered = lax.all_gather(packed, 'seg')]
    all_to_all x1 -> x0, waiting for transfers between devices: 125 us -> none  [body(): lax.all_to_all(outgoing, 'seg', split_axis=0, concat_axis=0, tiled=True)]
    psum x1 -> x0, waiting for transfers between devices: 81.2 us -> none  [body(): lax.psum(gram_local.astype(jnp.bfloat16), 'sub').astype(jnp.float32)]
    pallas_call x0 -> x2, Pallas kernels: none -> 37.5 us  [the longest x1 32.8 us: factors(): pl.pallas_call(factor_kernel, out_shape=(jax.ShapeDtypeStruct((n, n), jnp...]
    select_n x2 -> x0, local copies, waits for them, and re-layouts: 34 us -> none  [body(): jnp.where(jnp.transpose(routing, (2, 0, 1))[:, None, :, :, None], couplin...]
    all_to_all x1 -> x0, starting transfers between devices: 19.5 us -> none  [body(): lax.all_to_all(outgoing, 'seg', split_axis=0, concat_axis=0, tiled=True)]
    another operation x12 -> x0, local copies, waits for them, and re-layouts: 18.4 us -> none  [the longest x2 9.36 us: body(): couplings[0, 0]]
  transfers between devices with their start and end apart: 7 -> 9, of which waited for: 5 -> 7; matrix products, arithmetic and copies ran while one was open for 10% -> 3% of each run, Pallas kernels for 0% -> 0%
where the time goes in v1:
time: 257 us; the launch traced here: 252 us
  waiting for transfers between devices  144 us (56%)
  Pallas kernels  37.5 us (15%)
  starting transfers between devices  37 us (14%)
  between operations  14.2 us (6%)
  local copies, waits for them, and re-layouts  8.79 us (3%)
  other arithmetic  6.55 us (3%)
  matrix products  3.83 us (1%)
    all_gather x1, waiting for transfers between devices, body(): gathered = lax.all_gather(packed, 'seg')  126 us
    pallas_call x1, Pallas kernels, factors(): pl.pallas_call(factor_kernel, out_shape=(jax.ShapeDtypeStruct((n, n), jnp...  32.8 us
    ppermute x6, starting transfers between devices, from_partner(): return lax.ppermute(value, axis, pairs)  26.9 us
    ppermute x6, waiting for transfers between devices, from_partner(): return lax.ppermute(value, axis, pairs)  18.3 us
    ppermute x1, starting transfers between devices, padded(): after = lax.ppermute(leading, axis, down)  5.47 us
  transfers between devices with their start and end apart: 9, of which 7 were waited for; matrix products, arithmetic and copies ran while one was open for 3% of the time, Pallas kernels for 0%

profile of v1, /device:TPU:1, one launch (start us, length us, event | category | flops | bytes accessed | tf_op | source)
XLA Modules:
  0.0 251.9 jit_solution(15914433042987853738)
XLA Ops:
  7.2 0.0 copy-start
  7.2 0.0 all-gather.3.cloned.1.call-start
  7.2 0.8 convert_bitcast_fusion
  8.1 1.2 convolution_convert_fusion
  9.2 0.6 fusion.11
  9.9 0.0 all-gather.3.cloned.1.call-update
  9.9 4.6 %collective-permute-start = (bf16[512,256]{1,0:T(8,128)(2,1)}, bf16[512,256]{1,0:T(8,128)(2,1)S(1)}, u32[]{:S(2)}, u32[]{:S(2)}) collective-permute-start(bf16[512,256]{1,0:T(8,128)(2,1)} %param.9), channel_id=1, source_target_pairs={{0,1},{1,2},{2,3},{3,4},{4,5},{5,6},{6,7},{7,8},{8,9},{9,10},{10,1... | collective-permute-start | bytes 786440 | tf_op jit(solution)/shard_map/ppermute | solution.py:170
  14.5 5.5 %collective-permute-start.1 = (bf16[512,256]{1,0:T(8,128)(2,1)}, bf16[512,256]{1,0:T(8,128)(2,1)}, u32[]{:S(2)}, u32[]{:S(2)}) collective-permute-start(bf16[512,256]{1,0:T(8,128)(2,1)} %param.9), channel_id=1, source_target_pairs={{1,0},{2,1},{3,2},{4,3},{5,4},{6,5},{7,6},{8,7},{9,8},{10,9},{11,1... | collective-permute-start | bytes 786440 | tf_op jit(solution)/shard_map/ppermute | solution.py:171
  20.0 0.7 compare_select_fusion
  20.7 0.1 reshape.39
  20.7 0.8 copy.12
  21.5 0.1 reshape.32.dest_ref
  21.7 0.7 broadcast_compare_fusion
  22.3 0.0 collective-permute-done
  22.3 0.0 copy-start.4
  22.3 0.7 copy-done.4
  23.0 0.0 collective-permute-done.1
  23.1 1.2 pad_maximum_fusion.1
  24.2 2.4 gather_fusion
  26.6 0.0 copy-done
  26.6 0.0 copy-start.3
  26.6 2.7 %fusion = f32[2,256,256,1]{1,2,3,0:T(8,128)S(1)} fusion(bf16[2,10,256,256]{3,2,1,0:T(8,128)(2,1)S(1)} %copy-done, bf16[2,10,256,256]{3,2,1,0:T(8,128)(2,1)} %bitcast.35, pred[2,10]{1,0:T(4,128)(4,1)S(1)} %broadcast_compare_fusion), kind=kOutput, calls=%fused_computation.1 | convolution fusion | flops 672399360 | bytes 5767188 | tf_op jit(solution)/shard_map/lkab,lkbs->las/dot_general | solution.py:217
  29.3 125.8 %all-gather.3.cloned.1.call-done = bf16[9216,256]{1,0:T(8,128)(2,1)} async-done(((bf16[144,256]{1,0:T(8,128)(2,1)}), bf16[9216,256]{1,0:T(8,128)(2,1)}) %all-gather.3.cloned.1.call-update) | async-done | bytes 4718608 | tf_op jit(solution)/shard_map/all_gather | solution.py:206
  155.2 1.0 slice.6
  156.1 1.2 convert_reduce_fusion
  157.4 0.1 reshape.36.source_ref
  157.5 0.0 copy-done.3
  157.5 0.0 copy-start.1
  157.5 2.3 copy-done.1
  159.9 0.0 copy-start.2
  159.9 1.2 copy-done.2
  161.1 4.7 %shard_map.103 = (bf16[512,256]{1,0:T(8,128)(2,1)}, bf16[256,256]{1,0:T(8,128)(2,1)S(1)}) custom-call(s32[128]{0:T(128)S(1)} %reshape.36.source_ref, s32[128]{0:T(128)S(1)} %reshape.32.dest_ref, bf16[64,144,256]{2,1,0:T(8,128)(2,1)S(1)} %bitcast.31, bf16[64,64,128]{2,1,0:T(8,128)(2,1)S(1)} %bitcast.32, bf16[2,64,256]{2,1,0:T(8,128)(2,1)S(1)} %copy-done.3, ...), custom_call_target="tpu_custom_call" | custom-call | tf_op jit(solution)/shard_map/pallas_call | solution.py:151
  165.8 11.8 %collective-permute-start.2 = (bf16[256,256]{1,0:T(8,128)(2,1)S(1)}, bf16[256,256]{1,0:T(8,128)(2,1)S(1)}, u32[]{:S(2)}, u32[]{:S(2)}) collective-permute-start(bf16[256,256]{1,0:T(8,128)(2,1)S(1)} %get-tuple-element.8), channel_id=1, source_target_pairs={{0,1},{1,0},{2,3},{3,2},{4,5},{5,4},{6,7},{7,6},{8,9},{9,8},{10,11... | collective-permute-start | bytes 393224 | tf_op jit(solution)/shard_map/ppermute | solution.py:179
  177.5 1.0 collective-permute-done.2
  178.5 3.0 %collective-permute-start.3 = (bf16[256,256]{1,0:T(8,128)(2,1)S(1)}, bf16[256,256]{1,0:T(8,128)(2,1)S(1)}, u32[]{:S(2)}, u32[]{:S(2)}) collective-permute-start(bf16[256,256]{1,0:T(8,128)(2,1)S(1)} %add_convert_fusion.1), channel_id=1, source_target_pairs={{0,2},{1,3},{2,0},{3,1},{4,6},{5,7},{6,4},{7,5},{8,10},{9,11},{10,... | collective-permute-start | bytes 393224 | tf_op jit(solution)/shard_map/ppermute | solution.py:179
  181.6 3.6 %collective-permute-done.3 = bf16[256,256]{1,0:T(8,128)(2,1)S(1)} collective-permute-done((bf16[256,256]{1,0:T(8,128)(2,1)S(1)}, bf16[256,256]{1,0:T(8,128)(2,1)S(1)}, u32[]{:S(2)}, u32[]{:S(2)}) %collective-permute-start.3) | collective-permute-done | bytes 131104 | tf_op jit(solution)/shard_map/ppermute | solution.py:179
  185.2 4.6 %collective-permute-start.4 = (bf16[256,256]{1,0:T(8,128)(2,1)S(1)}, bf16[256,256]{1,0:T(8,128)(2,1)S(1)}, u32[]{:S(2)}, u32[]{:S(2)}) collective-permute-start(bf16[256,256]{1,0:T(8,128)(2,1)S(1)} %add_convert_fusion), channel_id=1, source_target_pairs={{0,4},{1,5},{2,6},{3,7},{4,0},{5,1},{6,2},{7,3},{8,12},{9,13},{10,... | collective-permute-start | bytes 393224 | tf_op jit(solution)/shard_map/ppermute | solution.py:179
  189.8 2.6 %collective-permute-done.4 = bf16[256,256]{1,0:T(8,128)(2,1)S(1)} collective-permute-done((bf16[256,256]{1,0:T(8,128)(2,1)S(1)}, bf16[256,256]{1,0:T(8,128)(2,1)S(1)}, u32[]{:S(2)}, u32[]{:S(2)}) %collective-permute-start.4) | collective-permute-done | bytes 131104 | tf_op jit(solution)/shard_map/ppermute | solution.py:179
  192.4 1.9 collective-permute-start.5
  194.4 3.8 %collective-permute-done.5 = bf16[256,256]{1,0:T(8,128)(2,1)S(1)} collective-permute-done((bf16[256,256]{1,0:T(8,128)(2,1)S(1)}, bf16[256,256]{1,0:T(8,128)(2,1)S(1)}, u32[]{:S(2)}, u32[]{:S(2)}) %collective-permute-start.5) | collective-permute-done | bytes 131104 | tf_op jit(solution)/shard_map/ppermute | solution.py:179
  198.2 2.6 %collective-permute-start.6 = (bf16[256,256]{1,0:T(8,128)(2,1)S(1)}, bf16[256,256]{1,0:T(8,128)(2,1)S(1)}, u32[]{:S(2)}, u32[]{:S(2)}) collective-permute-start(bf16[256,256]{1,0:T(8,128)(2,1)S(1)} %get-tuple-element.14), channel_id=1, source_target_pairs={{0,16},{8,24},{16,0},{24,8},{32,48},{40,56},{48,32},{56,40},{64,80... | collective-permute-start | bytes 393224 | tf_op jit(solution)/shard_map/ppermute | solution.py:179
  200.8 4.6 %collective-permute-done.6 = bf16[256,256]{1,0:T(8,128)(2,1)S(1)} collective-permute-done((bf16[256,256]{1,0:T(8,128)(2,1)S(1)}, bf16[256,256]{1,0:T(8,128)(2,1)S(1)}, u32[]{:S(2)}, u32[]{:S(2)}) %collective-permute-start.6) | collective-permute-done | bytes 131104 | tf_op jit(solution)/shard_map/ppermute | solution.py:179
  205.5 3.0 %collective-permute-start.7 = (bf16[256,256]{1,0:T(8,128)(2,1)S(1)}, bf16[256,256]{1,0:T(8,128)(2,1)S(1)}, u32[]{:S(2)}, u32[]{:S(2)}) collective-permute-start(bf16[256,256]{1,0:T(8,128)(2,1)S(1)} %get-tuple-element.16), channel_id=1, source_target_pairs={{0,32},{8,40},{16,48},{24,56},{32,0},{40,8},{48,16},{56,24},{64,96... | collective-permute-start | bytes 393224 | tf_op jit(solution)/shard_map/ppermute | solution.py:179
  208.5 2.7 %collective-permute-done.7 = bf16[256,256]{1,0:T(8,128)(2,1)S(1)} collective-permute-done((bf16[256,256]{1,0:T(8,128)(2,1)S(1)}, bf16[256,256]{1,0:T(8,128)(2,1)S(1)}, u32[]{:S(2)}, u32[]{:S(2)}) %collective-permute-start.7) | collective-permute-done | bytes 131104 | tf_op jit(solution)/shard_map/ppermute | solution.py:179
  211.2 1.1 pad_maximum_fusion.gram_ref
  212.3 32.8 %shard_map.104 = (f32[256,256]{1,0:T(8,128)}, bf16[3,256,256]{2,1,0:T(8,128)(2,1)}) custom-call(f32[4,256,256]{2,1,0:T(8,128)} %pad_maximum_fusion.gram_ref), custom_call_target="tpu_custom_call" | custom-call | tf_op jit(solution)/shard_map/pallas_call | solution.py:78
  (7 shorter events, 0.3 us)
Async XLA Ops:
  7.2 19.5 %copy-start = (bf16[2,10,256,256]{3,2,1,0:T(8,128)(2,1)S(1)}, bf16[2,10,256,256]{3,2,1,0:T(8,128)(2,1)}, u32[]{:S(2)}) copy-start(bf16[2,10,256,256]{3,2,1,0:T(8,128)(2,1)} %param.8) | copy-start | bytes 7864324
  7.2 148.0 %all-gather.3.cloned.1.call-start = ((), (), s32[]{:S(2)}) async-start(), calls=%async_computation | async-start | bytes 4792320 | tf_op jit(solution)/shard_map/all_gather | solution.py:206
  9.9 12.5 %collective-permute-start = (bf16[512,256]{1,0:T(8,128)(2,1)}, bf16[512,256]{1,0:T(8,128)(2,1)S(1)}, u32[]{:S(2)}, u32[]{:S(2)}) collective-permute-start(bf16[512,256]{1,0:T(8,128)(2,1)} %param.9), channel_id=1, source_target_pairs={{0,1},{1,2},{2,3},{3,4},{4,5},{5,6},{6,7},{7,8},{8,9},{9,10},{10,1... | collective-permute-start | bytes 786440 | tf_op jit(solution)/shard_map/ppermute | solution.py:170
  14.5 8.6 %collective-permute-start.1 = (bf16[512,256]{1,0:T(8,128)(2,1)}, bf16[512,256]{1,0:T(8,128)(2,1)}, u32[]{:S(2)}, u32[]{:S(2)}) collective-permute-start(bf16[512,256]{1,0:T(8,128)(2,1)} %param.9), channel_id=1, source_target_pairs={{1,0},{2,1},{3,2},{4,3},{5,4},{6,5},{7,6},{8,7},{9,8},{10,9},{11,1... | collective-permute-start | bytes 786440 | tf_op jit(solution)/shard_map/ppermute | solution.py:171
  22.3 0.7 copy-start.4
  26.6 130.9 %copy-start.3 = (bf16[2,64,256]{2,1,0:T(8,128)(2,1)S(1)}, bf16[2,64,256]{2,1,0:T(8,128)(2,1)}, u32[]{:S(2)}) copy-start(bf16[2,64,256]{2,1,0:T(8,128)(2,1)} %basis_ref.1) | copy-start | bytes 196612
  157.5 2.3 copy-start.1
  159.9 1.2 copy-start.2
  165.8 12.7 %collective-permute-start.2 = (bf16[256,256]{1,0:T(8,128)(2,1)S(1)}, bf16[256,256]{1,0:T(8,128)(2,1)S(1)}, u32[]{:S(2)}, u32[]{:S(2)}) collective-permute-start(bf16[256,256]{1,0:T(8,128)(2,1)S(1)} %get-tuple-element.8), channel_id=1, source_target_pairs={{0,1},{1,0},{2,3},{3,2},{4,5},{5,4},{6,7},{7,6},{8,9},{9,8},{10,11... | collective-permute-start | bytes 393224 | tf_op jit(solution)/shard_map/ppermute | solution.py:179
  178.5 6.6 %collective-permute-start.3 = (bf16[256,256]{1,0:T(8,128)(2,1)S(1)}, bf16[256,256]{1,0:T(8,128)(2,1)S(1)}, u32[]{:S(2)}, u32[]{:S(2)}) collective-permute-start(bf16[256,256]{1,0:T(8,128)(2,1)S(1)} %add_convert_fusion.1), channel_id=1, source_target_pairs={{0,2},{1,3},{2,0},{3,1},{4,6},{5,7},{6,4},{7,5},{8,10},{9,11},{10,... | collective-permute-start | bytes 393224 | tf_op jit(solution)/shard_map/ppermute | solution.py:179
  185.2 7.2 %collective-permute-start.4 = (bf16[256,256]{1,0:T(8,128)(2,1)S(1)}, bf16[256,256]{1,0:T(8,128)(2,1)S(1)}, u32[]{:S(2)}, u32[]{:S(2)}) collective-permute-start(bf16[256,256]{1,0:T(8,128)(2,1)S(1)} %add_convert_fusion), channel_id=1, source_target_pairs={{0,4},{1,5},{2,6},{3,7},{4,0},{5,1},{6,2},{7,3},{8,12},{9,13},{10,... | collective-permute-start | bytes 393224 | tf_op jit(solution)/shard_map/ppermute | solution.py:179
  192.4 5.7 %collective-permute-start.5 = (bf16[256,256]{1,0:T(8,128)(2,1)S(1)}, bf16[256,256]{1,0:T(8,128)(2,1)S(1)}, u32[]{:S(2)}, u32[]{:S(2)}) collective-permute-start(bf16[256,256]{1,0:T(8,128)(2,1)S(1)} %get-tuple-element.12), channel_id=1, source_target_pairs={{0,8},{8,0},{16,24},{24,16},{32,40},{40,32},{48,56},{56,48},{64,72... | collective-permute-start | bytes 393224 | tf_op jit(solution)/shard_map/ppermute | solution.py:179
  198.2 7.2 %collective-permute-start.6 = (bf16[256,256]{1,0:T(8,128)(2,1)S(1)}, bf16[256,256]{1,0:T(8,128)(2,1)S(1)}, u32[]{:S(2)}, u32[]{:S(2)}) collective-permute-start(bf16[256,256]{1,0:T(8,128)(2,1)S(1)} %get-tuple-element.14), channel_id=1, source_target_pairs={{0,16},{8,24},{16,0},{24,8},{32,48},{40,56},{48,32},{56,40},{64,80... | collective-permute-start | bytes 393224 | tf_op jit(solution)/shard_map/ppermute | solution.py:179
  205.5 5.7 %collective-permute-start.7 = (bf16[256,256]{1,0:T(8,128)(2,1)S(1)}, bf16[256,256]{1,0:T(8,128)(2,1)S(1)}, u32[]{:S(2)}, u32[]{:S(2)}) collective-permute-start(bf16[256,256]{1,0:T(8,128)(2,1)S(1)} %get-tuple-element.16), channel_id=1, source_target_pairs={{0,32},{8,40},{16,48},{24,56},{32,0},{40,8},{48,16},{56,24},{64,96... | collective-permute-start | bytes 393224 | tf_op jit(solution)/shard_map/ppermute | solution.py:179
Sparse Core Ops, SparseCore 0:
  11.5 143.5 all-gather.2

commit v2 on v1

--- a/solution.py
+++ b/solution.py
@@ -90,6 +90,171 @@
     )(stacked)
 
 
+SIDE = 4
+PLUS, MINUS = 0, 1
+
+
+def gather_kernel(own_ref, out_ref, own_sem, near_sems, ring_sems, line_sems, relay_sems):
+    seg_count, rows, _ = out_ref.shape
+    depth = seg_count // SIDE
+    half = depth // 2
+    me = lax.axis_index("seg")
+    z, x = me // SIDE, lax.rem(me, SIDE)
+    early = pl.ds(0, rows // 48 * 16)
+    late = pl.ds(rows // 48 * 16, rows - rows // 48 * 16)
+    sign = (1, -1)
+    reach = (half, half - 1)
+
+    def place(dz, dx):
+        return lax.rem(z + dz + depth, depth) * SIDE + lax.rem(x + dx + SIDE, SIDE)
+
+    def send(dz, dx, part, sems, target, own):
+        source = own_ref.at[part] if own else out_ref.at[place(dz, dx), part]
+        return pltpu.make_async_remote_copy(
+            src_ref=source,
+            dst_ref=out_ref.at[place(dz, dx), part],
+            send_sem=sems.at[0],
+            recv_sem=sems.at[1],
+            device_id={"seg": target},
+            device_id_type=pl.DeviceIdType.MESH,
+        )
+
+    def along_x(way):
+        return place(0, sign[way])
+
+    def along_z(way):
+        return place(sign[way], 0)
+
+    def near(way):
+        return send(0, 0, early, near_sems.at[way], along_x(way), True)
+
+    def near_relay():
+        return send(0, -1, early, near_sems.at[2], along_x(PLUS), False)
+
+    def ring(stream, way, hop, own=False):
+        part, dx = (late, 0) if stream == SIDE else (early, stream)
+        return send(
+            -sign[way] * (hop - 1), dx, part, ring_sems.at[stream, way, hop], along_z(way), own
+        )
+
+    def line(hop, way, side, own=False):
+        return send(-sign[way] * hop, 0, late, line_sems.at[hop, way, side], along_x(side), own)
+
+    def relay(hop, way, side):
+        return send(-sign[way] * hop, -sign[side], late, relay_sems.at[hop, way], along_x(side), False)
+
+    def pass_on(hop, way, side):
+        line(hop, way, side).wait_recv()
+        relay(hop, way, side).start()
+
+    def advance(stream, way, hop, further):
+        ring(stream, way, hop).wait_recv()
+        if further:
+            ring(stream, way, hop + 1).start()
+
+    def turn(hop, ways, further, streams):
+        for way in ways:
+            advance(SIDE, way, hop, way in further)
+            for side in (PLUS, MINUS):
+                line(hop, way, side).start()
+        for stream in streams:
+            for way in ways:
+                advance(stream, way, hop, way in further)
+
+    barrier = pltpu.get_barrier_semaphore()
+    for way in (PLUS, MINUS):
+        for target in (along_x(way), along_z(way)):
+            pl.semaphore_signal(
+                barrier, inc=1, device_id={"seg": target}, device_id_type=pl.DeviceIdType.MESH
+            )
+    pl.semaphore_wait(barrier, 4)
+
+    keep = pltpu.make_async_copy(own_ref, out_ref.at[me], own_sem)
+    keep.start()
+    for way in (PLUS, MINUS):
+        near(way).start()
+        ring(SIDE, way, 1, True).start()
+    for way in (PLUS, MINUS):
+        ring(0, way, 1, True).start()
+        line(0, PLUS, way, True).start()
+    both = (PLUS, MINUS)
+    for way, stream in ((PLUS, SIDE - 1), (MINUS, 1)):
+        near(way).wait_recv()
+        if way == PLUS:
+            near_relay().start()
+        for side in both:
+            ring(stream, side, 1).start()
+    turn(1, both, both, (0, SIDE - 1, 1))
+    near_relay().wait_recv()
+    for side in both:
+        ring(2, side, 1).start()
+    pass_on(0, PLUS, PLUS)
+    for way in both:
+        advance(2, way, 1, True)
+
+    def middle(hop, carry):
+        turn(hop, both, both, (0, SIDE - 1, 1, 2))
+        for way in both:
+            pass_on(hop - 1, way, way)
+        return carry
+
+    lax.fori_loop(2, half - 1, middle, 0)
+    turn(half - 1, both, (PLUS,), (0, SIDE - 1, 1, 2))
+    for way in both:
+        pass_on(half - 2, way, way)
+    turn(half, (PLUS,), (), (0, SIDE - 1, 1, 2))
+    for way in both:
+        pass_on(half - 1, way, way)
+    pass_on(half, PLUS, MINUS)
+
+    def finish(hop, way, side):
+        line(hop, way, 1 - side).wait_recv()
+        relay(hop, way, side).wait_recv()
+        for out in both:
+            line(hop, way, out).wait_send()
+        relay(hop, way, side).wait_send()
+
+    def drain(hop, carry):
+        for way in both:
+            finish(hop, way, way)
+            for stream in range(SIDE + 1):
+                ring(stream, way, hop).wait_send()
+        return carry
+
+    finish(0, PLUS, PLUS)
+    lax.fori_loop(1, half, drain, 0)
+    finish(half, PLUS, MINUS)
+    for stream in range(SIDE + 1):
+        ring(stream, PLUS, half).wait_send()
+    for way in both:
+        near(way).wait_send()
+    near_relay().wait_send()
+    keep.wait()
+
+
+def gather_segments(value):
+    rows, width = value.shape
+    seg_count = lax.axis_size("seg")
+    half = seg_count // SIDE // 2
+    dma = pltpu.SemaphoreType.DMA
+    return pl.pallas_call(
+        gather_kernel,
+        out_shape=jax.ShapeDtypeStruct((seg_count, rows, width), value.dtype),
+        in_specs=[pl.BlockSpec(memory_space=pltpu.VMEM)],
+        out_specs=pl.BlockSpec(memory_space=pltpu.VMEM),
+        scratch_shapes=[
+            dma,
+            dma((3, 2)),
+            dma((SIDE + 1, 2, half + 1, 2)),
+            dma((half + 1, 2, 2, 2)),
+            dma((half + 1, 2, 2)),
+        ],
+        compiler_params=pltpu.CompilerParams(
+            collective_id=0, has_side_effects=True, vmem_limit_bytes=32 * 2**20
+        ),
+    )(value)
+
+
 FAR_UNROLL = 4
 
 
@@ -203,7 +368,7 @@
     packed = jnp.concatenate(
         [basis_projector.reshape(leaf_count * rank_width, sample_width), source_rows], axis=0
     )
-    gathered = lax.all_gather(packed, "seg")
+    gathered = gather_segments(packed)
     sources = gathered[:, leaf_count * rank_width : leaf_count * rank_width + slot_number_count, :]
     sources = lax.dynamic_slice_in_dim(sources, lax.axis_index("seg"), 1, axis=2)
     sources = sources.astype(jnp.int32).reshape(seg_count * slot_number_count)

time: 257 us -> 160 us (0.62)
  the two profiles are of different devices: /device:TPU:1 before, /device:TPU:4 now
where the time goes in v2:
time: 160 us
  Pallas kernels  92 us (58%)
  waiting for transfers between devices  29.4 us (18%)
  starting transfers between devices  19.6 us (12%)
  local copies, waits for them, and re-layouts  8.75 us (5%)
  other arithmetic  5.07 us (3%)
  matrix products  3.89 us (2%)
    pallas_call x1, Pallas kernels, gather_segments(): pl.pallas_call(gather_kernel, out_shape=jax.ShapeDtypeStruct((seg_count,...  54.5 us
    pallas_call x1, Pallas kernels, factors(): pl.pallas_call(factor_kernel, out_shape=(jax.ShapeDtypeStruct((n, n), jnp...  32.8 us
    ppermute x6, waiting for transfers between devices, from_partner(): return lax.ppermute(value, axis, pairs)  29.4 us
    ppermute x6, starting transfers between devices, from_partner(): return lax.ppermute(value, axis, pairs)  11.7 us
    unnamed x15, local copies, waits for them, and re-layouts  5.94 us
    ppermute x1, starting transfers between devices, padded(): after = lax.ppermute(leading, axis, down)  5.75 us
    pallas_call x1, Pallas kernels, far_and_gram(): pl.pallas_call(far_kernel, out_shape=(jax.ShapeDtypeStruct((rows, width),...  4.67 us
  transfers between devices with their start and end apart: 8, of which 6 were waited for; matrix products, arithmetic and copies ran while one was open for 3% of the time, Pallas kernels for 34%

profile of v2, /device:TPU:4, one launch (start us, length us, event | category | flops | bytes accessed | tf_op | source)
XLA Modules:
  0.0 159.6 jit_solution(2269241031378981824)
XLA Ops:
  0.6 0.0 copy-start
  0.6 2.2 %collective-permute-start = (bf16[512,256]{1,0:T(8,128)(2,1)}, bf16[512,256]{1,0:T(8,128)(2,1)S(1)}, u32[]{:S(2)}, u32[]{:S(2)}) collective-permute-start(bf16[512,256]{1,0:T(8,128)(2,1)} %param.9), channel_id=1, source_target_pairs={{0,1},{1,2},{2,3},{3,4},{4,5},{5,6},{6,7},{7,8},{8,9},{9,10},{10,1... | collective-permute-start | bytes 786440 | tf_op jit(solution)/shard_map/ppermute | solution.py:335
  2.8 5.8 %collective-permute-start.1 = (bf16[512,256]{1,0:T(8,128)(2,1)}, bf16[512,256]{1,0:T(8,128)(2,1)}, u32[]{:S(2)}, u32[]{:S(2)}) collective-permute-start(bf16[512,256]{1,0:T(8,128)(2,1)} %param.9), channel_id=1, source_target_pairs={{1,0},{2,1},{3,2},{4,3},{5,4},{6,5},{7,6},{8,7},{9,8},{10,9},{11,1... | collective-permute-start | bytes 786440 | tf_op jit(solution)/shard_map/ppermute | solution.py:336
  8.6 0.7 convert_bitcast_fusion
  9.3 0.7 compare_select_fusion
  10.0 0.1 reshape.39
  10.1 1.2 convolution_convert_fusion
  11.2 0.0 copy-start.6
  11.3 0.8 copy.12
  12.0 0.1 reshape.32.dest_ref
  12.2 54.5 %shard_map.103.gathered_ref = bf16[64,144,256]{2,1,0:T(8,128)(2,1)S(1)} custom-call(bf16[144,256]{1,0:T(8,128)(2,1)S(1)} %fusion.11.own_ref), custom_call_target="tpu_custom_call" | custom-call | tf_op jit(solution)/shard_map/pallas_call | solution.py:240
  66.7 0.0 copy-start.1
  66.7 2.1 %copy-done.1 = bf16[64,144,256]{2,1,0:T(8,128)(2,1)} copy-done((bf16[64,144,256]{2,1,0:T(8,128)(2,1)}, bf16[64,144,256]{2,1,0:T(8,128)(2,1)S(1)}, u32[]{:S(2)}) %copy-start.1) | copy-done | bytes 4718616
  68.8 1.2 convert_reduce_fusion
  70.0 0.1 reshape.36.source_ref
  70.2 0.0 copy-done.6
  70.2 0.0 collective-permute-done
  70.2 0.0 copy-start.5
  70.2 0.7 copy-done.5
  70.9 0.0 collective-permute-done.1
  70.9 1.2 pad_maximum_fusion.1
  72.1 2.4 %gather_fusion = bf16[20,256,256]{2,1,0:T(8,128)(2,1)} fusion(bf16[6,256,256]{2,1,0:T(8,128)(2,1)S(1)} %bitcast.31, s32[1024]{0:T(1024)S(1)} %pad_clamp_fusion), kind=kCustom, calls=%fused_computation | custom fusion | bytes 5242960 | tf_op jit(solution)/shard_map/gather | solution.py:380
  74.5 0.0 copy-done
  74.5 0.0 copy-start.3
  74.5 0.0 copy-start.4
  74.5 2.7 %fusion = f32[2,256,256,1]{1,2,3,0:T(8,128)S(1)} fusion(bf16[2,10,256,256]{3,2,1,0:T(8,128)(2,1)S(1)} %copy-done, bf16[2,10,256,256]{3,2,1,0:T(8,128)(2,1)} %bitcast.32, pred[2,10]{1,0:T(4,128)(4,1)S(1)} %broadcast_compare_fusion), kind=kOutput, calls=%fused_computation.1 | convolution fusion | flops 672399360 | bytes 5767188 | tf_op jit(solution)/shard_map/lkab,lkbs->las/dot_general | solution.py:382
  77.3 0.0 copy-done.3
  77.3 0.0 copy-done.4
  77.3 0.0 copy-start.2
  77.3 2.3 %copy-done.2 = bf16[64,144,256]{2,1,0:T(8,128)(2,1)S(1)} copy-done((bf16[64,144,256]{2,1,0:T(8,128)(2,1)S(1)}, bf16[64,144,256]{2,1,0:T(8,128)(2,1)}, u32[]{:S(2)}) %copy-start.2) | copy-done | bytes 4718616
  79.6 4.7 %shard_map.104 = (bf16[512,256]{1,0:T(8,128)(2,1)}, bf16[256,256]{1,0:T(8,128)(2,1)S(1)}) custom-call(s32[128]{0:T(128)S(1)} %reshape.36.source_ref, s32[128]{0:T(128)S(1)} %reshape.32.dest_ref, bf16[64,144,256]{2,1,0:T(8,128)(2,1)S(1)} %copy-done.2, bf16[64,64,128]{2,1,0:T(8,128)(2,1)S(1)} %bitcast.29, bf16[2,64,256]{2,1,0:T(8,128)(2,1)S(1)} %copy-done.4, ...), custom_call_target="tpu_custom_call" | custom-call | tf_op jit(solution)/shard_map/pallas_call | solution.py:316
  84.3 1.9 %collective-permute-start.2 = (bf16[256,256]{1,0:T(8,128)(2,1)S(1)}, bf16[256,256]{1,0:T(8,128)(2,1)S(1)}, u32[]{:S(2)}, u32[]{:S(2)}) collective-permute-start(bf16[256,256]{1,0:T(8,128)(2,1)S(1)} %get-tuple-element.8), channel_id=1, source_target_pairs={{0,1},{1,0},{2,3},{3,2},{4,5},{5,4},{6,7},{7,6},{8,9},{9,8},{10,11... | collective-permute-start | bytes 393224 | tf_op jit(solution)/shard_map/ppermute | solution.py:344
  86.2 1.3 collective-permute-done.2
  87.6 1.9 %collective-permute-start.3 = (bf16[256,256]{1,0:T(8,128)(2,1)S(1)}, bf16[256,256]{1,0:T(8,128)(2,1)S(1)}, u32[]{:S(2)}, u32[]{:S(2)}) collective-permute-start(bf16[256,256]{1,0:T(8,128)(2,1)S(1)} %add_convert_fusion.1), channel_id=1, source_target_pairs={{0,2},{1,3},{2,0},{3,1},{4,6},{5,7},{6,4},{7,5},{8,10},{9,11},{10,... | collective-permute-start | bytes 393224 | tf_op jit(solution)/shard_map/ppermute | solution.py:344
  89.5 5.5 %collective-permute-done.3 = bf16[256,256]{1,0:T(8,128)(2,1)S(1)} collective-permute-done((bf16[256,256]{1,0:T(8,128)(2,1)S(1)}, bf16[256,256]{1,0:T(8,128)(2,1)S(1)}, u32[]{:S(2)}, u32[]{:S(2)}) %collective-permute-start.3) | collective-permute-done | bytes 131104 | tf_op jit(solution)/shard_map/ppermute | solution.py:344
  95.0 1.9 %collective-permute-start.4 = (bf16[256,256]{1,0:T(8,128)(2,1)S(1)}, bf16[256,256]{1,0:T(8,128)(2,1)S(1)}, u32[]{:S(2)}, u32[]{:S(2)}) collective-permute-start(bf16[256,256]{1,0:T(8,128)(2,1)S(1)} %add_convert_fusion), channel_id=1, source_target_pairs={{0,4},{1,5},{2,6},{3,7},{4,0},{5,1},{6,2},{7,3},{8,12},{9,13},{10,... | collective-permute-start | bytes 393224 | tf_op jit(solution)/shard_map/ppermute | solution.py:344
  97.0 6.4 %collective-permute-done.4 = bf16[256,256]{1,0:T(8,128)(2,1)S(1)} collective-permute-done((bf16[256,256]{1,0:T(8,128)(2,1)S(1)}, bf16[256,256]{1,0:T(8,128)(2,1)S(1)}, u32[]{:S(2)}, u32[]{:S(2)}) %collective-permute-start.4) | collective-permute-done | bytes 131104 | tf_op jit(solution)/shard_map/ppermute | solution.py:344
  103.5 1.9 %collective-permute-start.5 = (bf16[256,256]{1,0:T(8,128)(2,1)S(1)}, bf16[256,256]{1,0:T(8,128)(2,1)S(1)}, u32[]{:S(2)}, u32[]{:S(2)}) collective-permute-start(bf16[256,256]{1,0:T(8,128)(2,1)S(1)} %get-tuple-element.12), channel_id=1, source_target_pairs={{0,8},{8,0},{16,24},{24,16},{32,40},{40,32},{48,56},{56,48},{64,72... | collective-permute-start | bytes 393224 | tf_op jit(solution)/shard_map/ppermute | solution.py:344
  105.4 4.9 %collective-permute-done.5 = bf16[256,256]{1,0:T(8,128)(2,1)S(1)} collective-permute-done((bf16[256,256]{1,0:T(8,128)(2,1)S(1)}, bf16[256,256]{1,0:T(8,128)(2,1)S(1)}, u32[]{:S(2)}, u32[]{:S(2)}) %collective-permute-start.5) | collective-permute-done | bytes 131104 | tf_op jit(solution)/shard_map/ppermute | solution.py:344
  110.4 1.9 %collective-permute-start.6 = (bf16[256,256]{1,0:T(8,128)(2,1)S(1)}, bf16[256,256]{1,0:T(8,128)(2,1)S(1)}, u32[]{:S(2)}, u32[]{:S(2)}) collective-permute-start(bf16[256,256]{1,0:T(8,128)(2,1)S(1)} %get-tuple-element.14), channel_id=1, source_target_pairs={{0,16},{8,24},{16,0},{24,8},{32,48},{40,56},{48,32},{56,40},{64,80... | collective-permute-start | bytes 393224 | tf_op jit(solution)/shard_map/ppermute | solution.py:344
  112.3 6.4 %collective-permute-done.6 = bf16[256,256]{1,0:T(8,128)(2,1)S(1)} collective-permute-done((bf16[256,256]{1,0:T(8,128)(2,1)S(1)}, bf16[256,256]{1,0:T(8,128)(2,1)S(1)}, u32[]{:S(2)}, u32[]{:S(2)}) %collective-permute-start.6) | collective-permute-done | bytes 131104 | tf_op jit(solution)/shard_map/ppermute | solution.py:344
  118.8 2.1 %collective-permute-start.7 = (bf16[256,256]{1,0:T(8,128)(2,1)S(1)}, bf16[256,256]{1,0:T(8,128)(2,1)S(1)}, u32[]{:S(2)}, u32[]{:S(2)}) collective-permute-start(bf16[256,256]{1,0:T(8,128)(2,1)S(1)} %get-tuple-element.16), channel_id=1, source_target_pairs={{0,32},{8,40},{16,48},{24,56},{32,0},{40,8},{48,16},{56,24},{64,96... | collective-permute-start | bytes 393224 | tf_op jit(solution)/shard_map/ppermute | solution.py:344
  120.9 4.8 %collective-permute-done.7 = bf16[256,256]{1,0:T(8,128)(2,1)S(1)} collective-permute-done((bf16[256,256]{1,0:T(8,128)(2,1)S(1)}, bf16[256,256]{1,0:T(8,128)(2,1)S(1)}, u32[]{:S(2)}, u32[]{:S(2)}) %collective-permute-start.7) | collective-permute-done | bytes 131104 | tf_op jit(solution)/shard_map/ppermute | solution.py:344
  125.7 1.1 pad_maximum_fusion.gram_ref
  126.7 32.8 %shard_map.105 = (f32[256,256]{1,0:T(8,128)}, bf16[3,256,256]{2,1,0:T(8,128)(2,1)}) custom-call(f32[4,256,256]{2,1,0:T(8,128)} %pad_maximum_fusion.gram_ref), custom_call_target="tpu_custom_call" | custom-call | tf_op jit(solution)/shard_map/pallas_call | solution.py:78
  (10 shorter events, 0.3 us)
Async XLA Ops:
  0.6 73.9 %copy-start = (bf16[2,10,256,256]{3,2,1,0:T(8,128)(2,1)S(1)}, bf16[2,10,256,256]{3,2,1,0:T(8,128)(2,1)}, u32[]{:S(2)}) copy-start(bf16[2,10,256,256]{3,2,1,0:T(8,128)(2,1)} %param.8) | copy-start | bytes 7864324
  0.6 69.6 %collective-permute-start = (bf16[512,256]{1,0:T(8,128)(2,1)}, bf16[512,256]{1,0:T(8,128)(2,1)S(1)}, u32[]{:S(2)}, u32[]{:S(2)}) collective-permute-start(bf16[512,256]{1,0:T(8,128)(2,1)} %param.9), channel_id=1, source_target_pairs={{0,1},{1,2},{2,3},{3,4},{4,5},{5,6},{6,7},{7,8},{8,9},{9,10},{10,1... | collective-permute-start | bytes 786440 | tf_op jit(solution)/shard_map/ppermute | solution.py:335
  2.8 68.1 %collective-permute-start.1 = (bf16[512,256]{1,0:T(8,128)(2,1)}, bf16[512,256]{1,0:T(8,128)(2,1)}, u32[]{:S(2)}, u32[]{:S(2)}) collective-permute-start(bf16[512,256]{1,0:T(8,128)(2,1)} %param.9), channel_id=1, source_target_pairs={{1,0},{2,1},{3,2},{4,3},{5,4},{6,5},{7,6},{8,7},{9,8},{10,9},{11,1... | collective-permute-start | bytes 786440 | tf_op jit(solution)/shard_map/ppermute | solution.py:336
  11.2 59.0 %copy-start.6 = (s32[2,10]{1,0:T(2,128)S(1)}, s32[2,10]{1,0:T(2,128)}, u32[]{:S(2)}) copy-start(s32[2,10]{1,0:T(2,128)} %param.10) | copy-start | bytes 244
  66.7 2.1 %copy-start.1 = (bf16[64,144,256]{2,1,0:T(8,128)(2,1)}, bf16[64,144,256]{2,1,0:T(8,128)(2,1)S(1)}, u32[]{:S(2)}) copy-start(bf16[64,144,256]{2,1,0:T(8,128)(2,1)S(1)} %shard_map.103.gathered_ref) | copy-start | bytes 14155780
  70.2 0.7 copy-start.5
  74.5 2.8 %copy-start.3 = (bf16[1,1,64,64,128]{4,3,2,1,0:T(8,128)(2,1)S(1)}, bf16[1,1,64,64,128]{4,3,2,1,0:T(8,128)(2,1)}, u32[]{:S(2)}) copy-start(bf16[1,1,64,64,128]{4,3,2,1,0:T(8,128)(2,1)} %param.13) | copy-start | bytes 3145732
  74.5 2.8 %copy-start.4 = (bf16[2,64,256]{2,1,0:T(8,128)(2,1)S(1)}, bf16[2,64,256]{2,1,0:T(8,128)(2,1)}, u32[]{:S(2)}) copy-start(bf16[2,64,256]{2,1,0:T(8,128)(2,1)} %basis_ref.1) | copy-start | bytes 196612
  77.3 2.3 %copy-start.2 = (bf16[64,144,256]{2,1,0:T(8,128)(2,1)S(1)}, bf16[64,144,256]{2,1,0:T(8,128)(2,1)}, u32[]{:S(2)}) copy-start(bf16[64,144,256]{2,1,0:T(8,128)(2,1)} %copy-done.1) | copy-start | bytes 14155780
  84.3 3.2 %collective-permute-start.2 = (bf16[256,256]{1,0:T(8,128)(2,1)S(1)}, bf16[256,256]{1,0:T(8,128)(2,1)S(1)}, u32[]{:S(2)}, u32[]{:S(2)}) collective-permute-start(bf16[256,256]{1,0:T(8,128)(2,1)S(1)} %get-tuple-element.8), channel_id=1, source_target_pairs={{0,1},{1,0},{2,3},{3,2},{4,5},{5,4},{6,7},{7,6},{8,9},{9,8},{10,11... | collective-permute-start | bytes 393224 | tf_op jit(solution)/shard_map/ppermute | solution.py:344
  87.6 7.4 %collective-permute-start.3 = (bf16[256,256]{1,0:T(8,128)(2,1)S(1)}, bf16[256,256]{1,0:T(8,128)(2,1)S(1)}, u32[]{:S(2)}, u32[]{:S(2)}) collective-permute-start(bf16[256,256]{1,0:T(8,128)(2,1)S(1)} %add_convert_fusion.1), channel_id=1, source_target_pairs={{0,2},{1,3},{2,0},{3,1},{4,6},{5,7},{6,4},{7,5},{8,10},{9,11},{10,... | collective-permute-start | bytes 393224 | tf_op jit(solution)/shard_map/ppermute | solution.py:344
  95.0 8.4 %collective-permute-start.4 = (bf16[256,256]{1,0:T(8,128)(2,1)S(1)}, bf16[256,256]{1,0:T(8,128)(2,1)S(1)}, u32[]{:S(2)}, u32[]{:S(2)}) collective-permute-start(bf16[256,256]{1,0:T(8,128)(2,1)S(1)} %add_convert_fusion), channel_id=1, source_target_pairs={{0,4},{1,5},{2,6},{3,7},{4,0},{5,1},{6,2},{7,3},{8,12},{9,13},{10,... | collective-permute-start | bytes 393224 | tf_op jit(solution)/shard_map/ppermute | solution.py:344
  103.5 6.9 %collective-permute-start.5 = (bf16[256,256]{1,0:T(8,128)(2,1)S(1)}, bf16[256,256]{1,0:T(8,128)(2,1)S(1)}, u32[]{:S(2)}, u32[]{:S(2)}) collective-permute-start(bf16[256,256]{1,0:T(8,128)(2,1)S(1)} %get-tuple-element.12), channel_id=1, source_target_pairs={{0,8},{8,0},{16,24},{24,16},{32,40},{40,32},{48,56},{56,48},{64,72... | collective-permute-start | bytes 393224 | tf_op jit(solution)/shard_map/ppermute | solution.py:344
  110.4 8.4 %collective-permute-start.6 = (bf16[256,256]{1,0:T(8,128)(2,1)S(1)}, bf16[256,256]{1,0:T(8,128)(2,1)S(1)}, u32[]{:S(2)}, u32[]{:S(2)}) collective-permute-start(bf16[256,256]{1,0:T(8,128)(2,1)S(1)} %get-tuple-element.14), channel_id=1, source_target_pairs={{0,16},{8,24},{16,0},{24,8},{32,48},{40,56},{48,32},{56,40},{64,80... | collective-permute-start | bytes 393224 | tf_op jit(solution)/shard_map/ppermute | solution.py:344
  118.8 6.9 %collective-permute-start.7 = (bf16[256,256]{1,0:T(8,128)(2,1)S(1)}, bf16[256,256]{1,0:T(8,128)(2,1)S(1)}, u32[]{:S(2)}, u32[]{:S(2)}) collective-permute-start(bf16[256,256]{1,0:T(8,128)(2,1)S(1)} %get-tuple-element.16), channel_id=1, source_target_pairs={{0,32},{8,40},{16,48},{24,56},{32,0},{40,8},{48,16},{56,24},{64,96... | collective-permute-start | bytes 393224 | tf_op jit(solution)/shard_map/ppermute | solution.py:344

commit v3 on v2

--- a/solution.py
+++ b/solution.py
@@ -1,3 +1,5 @@
+import functools
+
 import jax
 import jax.numpy as jnp
 from jax import lax
@@ -50,7 +52,7 @@
 def factor_kernel(gram_ref, factor_ref, transfer_ref, work, upper):
     count, n, _ = work.shape
     lanes = lax.broadcasted_iota(jnp.int32, (1, n), 1)
-    work[...] = gram_ref[...]
+    work[...] = gram_ref[...].astype(jnp.float32)
     upper[...] = jnp.zeros_like(upper)
     for at in range(0, n, BLOCK):
         end = at + BLOCK
@@ -255,16 +257,154 @@
     )(value)
 
 
+def gram_kernel(rows_each, local_ref, out_ref, parts, sums, peers, reduce_sems, level_sems, share_sems, core_sems):
+    sub_count, chunk, _ = parts.shape
+    group = peers.shape[0]
+    me, seg = lax.axis_index("sub"), lax.axis_index("seg")
+    level_count = out_ref.shape[0]
+    share = 1.0 / (sub_count * rows_each)
+
+    def ahead(step):
+        return lax.rem(me + step, sub_count)
+
+    def partner(mask):
+        value = seg
+        for bit in range(mask.bit_length()):
+            if mask >> bit & 1:
+                value = value + 2**bit * (1 - 2 * lax.rem(seg // 2**bit, 2))
+        return value
+
+    def rows(device):
+        return pl.ds(pl.multiple_of(device * chunk, chunk), chunk)
+
+    def remote(source, target, sems, where):
+        return pltpu.make_async_remote_copy(
+            src_ref=source,
+            dst_ref=target,
+            send_sem=sems.at[0],
+            recv_sem=sems.at[1],
+            device_id=where,
+            device_id_type=pl.DeviceIdType.MESH,
+        )
+
+    barrier = pltpu.get_barrier_semaphore()
+    for step in range(1, sub_count):
+        pl.semaphore_signal(
+            barrier, inc=1, device_id={"sub": ahead(step)}, device_id_type=pl.DeviceIdType.MESH
+        )
+    for mask in range(1, group):
+        pl.semaphore_signal(
+            barrier, inc=1, device_id={"seg": partner(mask)}, device_id_type=pl.DeviceIdType.MESH
+        )
+    pl.semaphore_wait(barrier, sub_count + group - 2)
+
+    def reduce_copy(step):
+        return remote(
+            local_ref.at[rows(ahead(step))],
+            parts.at[step],
+            reduce_sems.at[step],
+            {"sub": ahead(step)},
+        )
+
+    def level_copy(mask):
+        return remote(sums, peers.at[mask], level_sems.at[mask], {"seg": partner(mask)})
+
+    for step in range(1, sub_count):
+        reduce_copy(step).start()
+    total = local_ref[rows(me), :].astype(jnp.float32)
+    for step in range(1, sub_count):
+        reduce_copy(step).wait_recv()
+        total = total + parts[step].astype(jnp.float32)
+    total = total * share
+    sums[...] = total.astype(sums.dtype)
+    for mask in range(1, group):
+        level_copy(mask).start()
+    out_ref[0, rows(me), :] = total.astype(out_ref.dtype)
+    for level in range(1, level_count):
+        for mask in range(2 ** (level - 1), 2**level):
+            level_copy(mask).wait_recv()
+            total = total + peers[mask].astype(jnp.float32)
+        out_ref[level, rows(me), :] = (total * 0.5**level).astype(out_ref.dtype)
+
+    core = lax.rem(me, 2)
+    other = me + 1 - 2 * core
+    spread = range(2, sub_count, 2)
+
+    def share_copy(step):
+        mine = out_ref.at[:, rows(me), :]
+        return remote(mine, mine, share_sems.at[step], {"sub": ahead(step)})
+
+    def core_copy(step):
+        block = out_ref.at[:, rows(lax.rem(me + sub_count - step, sub_count)), :]
+        return remote(block, block, core_sems.at[step], {"sub": other})
+
+    for step in spread:
+        share_copy(step).start()
+    core_copy(0).start()
+    for step in sorted(spread, key=lambda s: min(s, sub_count - s)):
+        share_copy(step).wait_recv()
+        core_copy(step).start()
+    for step in range(0, sub_count, 2):
+        core_copy(step).wait_recv()
+    for step in range(1, sub_count):
+        reduce_copy(step).wait_send()
+    for mask in range(1, group):
+        level_copy(mask).wait_send()
+    for step in spread:
+        share_copy(step).wait_send()
+    for step in range(0, sub_count, 2):
+        core_copy(step).wait_send()
+
+
+def level_grams(local, rows_each):
+    width = local.shape[0]
+    sub_count, group = lax.axis_size("sub"), 2**LEVELS
+    chunk = width // sub_count
+    dma = pltpu.SemaphoreType.DMA
+    return pl.pallas_call(
+        functools.partial(gram_kernel, rows_each),
+        out_shape=jax.ShapeDtypeStruct((LEVELS + 1, width, width), local.dtype),
+        in_specs=[pl.BlockSpec(memory_space=pltpu.VMEM)],
+        out_specs=pl.BlockSpec(memory_space=pltpu.VMEM),
+        scratch_shapes=[
+            pltpu.VMEM((sub_count, chunk, width), local.dtype),
+            pltpu.VMEM((chunk, width), local.dtype),
+            pltpu.VMEM((group, chunk, width), local.dtype),
+            dma((sub_count, 2)),
+            dma((group, 2)),
+            dma((sub_count, 2)),
+            dma((sub_count, 2)),
+        ],
+        compiler_params=pltpu.CompilerParams(collective_id=1, has_side_effects=True),
+    )(local)
+
+
 FAR_UNROLL = 4
 
 
 def far_kernel(
-    source_ref, dest_ref, gathered_ref, coupling_ref, basis_ref, near_ref, samples_ref, gram_ref
+    source_ref,
+    dest_ref,
+    position_ref,
+    gathered_ref,
+    coupling_ref,
+    basis_ref,
+    block_ref,
+    before_ref,
+    own_ref,
+    after_ref,
+    samples_ref,
+    gram_ref,
+    extended,
 ):
     leaf_count, rank, leaf_rows = basis_ref.shape
     seg_count = coupling_ref.shape[0]
     slots = coupling_ref.shape[2] // rank
     width = gathered_ref.shape[2]
+    near_count = block_ref.shape[1]
+    own_rows = own_ref.shape[0]
+    for index, part in enumerate((before_ref, own_ref, after_ref)):
+        extended[index * own_rows : (index + 1) * own_rows, :] = part[...]
     lane = lax.broadcasted_iota(jnp.int32, (1, slots * rank), 1) // rank
 
     def step(index, total):
@@ -303,15 +443,26 @@
             (((0,), (0,)), ((), ())),
             preferred_element_type=jnp.float32,
         )
-        samples_ref[rows, :] = (near_ref[rows, :] + far).astype(jnp.bfloat16)
+        picked = []
+        for entry in range(near_count):
+            position = position_ref[leaf * near_count + entry]
+            start = pl.multiple_of(jnp.maximum(position, 0) * leaf_rows, leaf_rows)
+            value = extended[pl.ds(start, leaf_rows), :]
+            picked.append(jnp.where(position >= 0, value, jnp.zeros_like(value)))
+        near = jnp.dot(
+            jnp.concatenate([block_ref[leaf, entry] for entry in range(near_count)], axis=1),
+            jnp.concatenate(picked, axis=0),
+            preferred_element_type=jnp.float32,
+        )
+        samples_ref[rows, :] = (near + far).astype(jnp.bfloat16)
     samples = samples_ref[...]
     gram_ref[...] = lax.dot_general(
         samples, samples, (((0,), (0,)), ((), ())), preferred_element_type=jnp.float32
     ).astype(gram_ref.dtype)
 
 
-def far_and_gram(source, dest, gathered, coupling, basis, near):
-    rows, width = near.shape
+def far_and_gram(source, dest, position, gathered, coupling, basis, blocks, before, own, after):
+    rows, width = own.shape
     smem, vmem = pl.BlockSpec(memory_space=pltpu.SMEM), pl.BlockSpec(memory_space=pltpu.VMEM)
     return pl.pallas_call(
         far_kernel,
@@ -319,34 +470,18 @@
             jax.ShapeDtypeStruct((rows, width), jnp.bfloat16),
             jax.ShapeDtypeStruct((width, width), jnp.bfloat16),
         ),
-        in_specs=[smem, smem, vmem, vmem, vmem, vmem],
+        in_specs=[smem] * 3 + [vmem] * 7,
         out_specs=[vmem, vmem],
+        scratch_shapes=[pltpu.VMEM((3 * rows, width), own.dtype)],
         compiler_params=pltpu.CompilerParams(vmem_limit_bytes=32 * 2**20),
-    )(source, dest, gathered, coupling, basis, near)
-
-
-def padded(value, sides, width):
-    for axis, dim in sides:
-        size, length = (lax.axis_size(axis), value.shape[dim])
-        up = [(i, (i + 1) % size) for i in range(size - 1)]
-        down = [(j, i) for i, j in up]
-        last = lax.slice_in_dim(value, length - width, length, axis=dim)
-        leading = lax.slice_in_dim(value, 0, width, axis=dim)
-        before = lax.ppermute(last, axis, up)
-        after = lax.ppermute(leading, axis, down)
-        value = jnp.concatenate([before, value, after], axis=dim)
-    return value
-
-
-def from_partner(value, axis, distance):
-    mask = 2**distance
-    pairs = [(source, source ^ mask) for source in range(lax.axis_size(axis))]
-    return lax.ppermute(value, axis, pairs)
-
-
-def paired_sum(value, axis, distance):
-    partner = from_partner(value, axis, distance)
-    return value.astype(jnp.float32) + partner.astype(jnp.float32)
+    )(source, dest, position, gathered, coupling, basis, blocks, before, own, after)
+
+
+def neighbours(value, axes):
+    size = lax.axis_size(axes)
+    up = [(i, i + 1) for i in range(size - 1)]
+    down = [(j, i) for i, j in up]
+    return (lax.ppermute(value, axes, up), lax.ppermute(value, axes, down))
 
 
 def body(
@@ -372,34 +507,22 @@
     sources = gathered[:, leaf_count * rank_width : leaf_count * rank_width + slot_number_count, :]
     sources = lax.dynamic_slice_in_dim(sources, lax.axis_index("seg"), 1, axis=2)
     sources = sources.astype(jnp.int32).reshape(seg_count * slot_number_count)
-    extended = padded(sample_cols, ((("seg", "sub"), 0),), leaf_count * leaf_rows)
-    extended = extended.reshape(3 * leaf_count, leaf_rows, sample_width)
+    before, after = neighbours(sample_cols, ("seg", "sub"))
     base_leaf = (lax.axis_index(("seg", "sub")) - 1) * leaf_count
-    usable = near_list >= 0
-    position = jnp.where(usable, near_list - base_leaf, 0)
-    chosen = extended[position]
-    chosen = jnp.where(usable[:, :, None, None], chosen, jnp.zeros_like(chosen))
-    near_part = jnp.einsum(
-        "lkab,lkbs->las", near_blocks, chosen, preferred_element_type=jnp.float32
-    )
+    position = jnp.where(near_list >= 0, near_list - base_leaf, -1)
     samples, gram_local = far_and_gram(
         sources,
         far_dest.reshape(seg_count * slot_number_count),
+        position.reshape(leaf_count * near_count),
         gathered,
         couplings[0, 0],
         row_basis_t,
-        near_part.reshape(leaf_count * leaf_rows, sample_width),
+        near_blocks,
+        before,
+        sample_cols,
+        after,
     )
-    row_total = lax.axis_size("sub") * leaf_count * leaf_rows
-    current = gram_local
-    for distance in range((lax.axis_size("sub") - 1).bit_length()):
-        total = paired_sum(current, "sub", distance)
-        current = total.astype(jnp.bfloat16)
-    gram_levels = [total / row_total]
-    for distance in range(LEVELS):
-        total = paired_sum(gram_levels[-1].astype(jnp.bfloat16), "seg", distance) * 0.5
-        gram_levels.append(total)
-    segment_factor, transfers = factors(jnp.stack(gram_levels))
+    segment_factor, transfers = factors(level_grams(gram_local, leaf_count * leaf_rows))
     return (samples, segment_factor, transfers[None])
 
 

time: 160 us -> 139 us (0.87)
  the two profiles are of different devices: /device:TPU:4 before, /device:TPU:1 now
where the time goes in v3:
time: 139 us; the launch traced here: 138 us
  Pallas kernels  112 us (81%)
  local copies, waits for them, and re-layouts  10.3 us (7%)
  starting transfers between devices  10.3 us (7%)
  other arithmetic  3.99 us (3%)
    pallas_call x1, Pallas kernels, gather_segments(): pl.pallas_call(gather_kernel, out_shape=jax.ShapeDtypeStruct((seg_count,...  42.1 us
    pallas_call x1, Pallas kernels, factors(): pl.pallas_call(factor_kernel, out_shape=(jax.ShapeDtypeStruct((n, n), jnp...  32.6 us
    pallas_call x1, Pallas kernels, level_grams(): pl.pallas_call(functools.partial(gram_kernel, rows_each), out_shape=jax.S...  31.4 us
    ppermute x2, starting transfers between devices, neighbours(): return (lax.ppermute(value, axes, up), lax.ppermute(value, axes, down))  10.3 us
    unnamed x17, local copies, waits for them, and re-layouts  7.74 us
    pallas_call x1, Pallas kernels, far_and_gram(): pl.pallas_call(far_kernel, out_shape=(jax.ShapeDtypeStruct((rows, width),...  5.57 us
  transfers between devices with their start and end apart: 2, of which 0 were waited for; matrix products, arithmetic and copies ran while one was open for 7% of the time, Pallas kernels for 30%

profile of v3, /device:TPU:1, one launch (start us, length us, event | category | flops | bytes accessed | tf_op | source)
XLA Modules:
  0.0 138.1 jit_solution(17697096297744754833)
XLA Ops:
  0.6 0.0 copy-start
  0.6 0.0 copy-start.5
  0.7 0.0 copy-start.7
  0.7 0.0 copy-start.3
  0.7 4.8 %collective-permute-start = (bf16[512,256]{1,0:T(8,128)(2,1)}, bf16[512,256]{1,0:T(8,128)(2,1)S(1)}, u32[]{:S(2)}, u32[]{:S(2)}) collective-permute-start(bf16[512,256]{1,0:T(8,128)(2,1)} %own_ref.1), channel_id=1, source_target_pairs={{0,1},{1,2},{2,3},{3,4},{4,5},{5,6},{6,7},{7,8},{8,9},{9,10},{10,1... | collective-permute-start | bytes 786440 | tf_op jit(solution)/shard_map/ppermute | solution.py:484
  5.5 5.5 %collective-permute-start.1 = (bf16[512,256]{1,0:T(8,128)(2,1)}, bf16[512,256]{1,0:T(8,128)(2,1)S(1)}, u32[]{:S(2)}, u32[]{:S(2)}) collective-permute-start(bf16[512,256]{1,0:T(8,128)(2,1)} %own_ref.1), channel_id=1, source_target_pairs={{1,0},{2,1},{3,2},{4,3},{5,4},{6,5},{7,6},{8,7},{9,8},{10,9},{11,1... | collective-permute-start | bytes 786440 | tf_op jit(solution)/shard_map/ppermute | solution.py:484
  11.0 0.7 compare_select_fusion
  11.7 0.1 reshape.29.position_ref
  11.8 1.4 copy.12
  13.2 0.9 reshape.28.dest_ref
  14.1 0.0 copy-done
  14.1 1.1 convolution_convert_fusion
  15.2 0.7 convert_bitcast_fusion
  15.9 42.1 %shard_map.103.gathered_ref = bf16[64,144,256]{2,1,0:T(8,128)(2,1)S(1)} custom-call(bf16[144,256]{1,0:T(8,128)(2,1)S(1)} %fusion.1.own_ref), custom_call_target="tpu_custom_call" | custom-call | tf_op jit(solution)/shard_map/pallas_call | solution.py:242
  58.0 0.7 slice.3
  58.6 0.0 copy-start.1
  58.6 2.1 %copy-done.1 = bf16[64,144,256]{2,1,0:T(8,128)(2,1)} copy-done((bf16[64,144,256]{2,1,0:T(8,128)(2,1)}, bf16[64,144,256]{2,1,0:T(8,128)(2,1)S(1)}, u32[]{:S(2)}) %copy-start.1) | copy-done | bytes 4718616
  60.8 2.6 %convert_reduce_fusion = s32[64,2]{1,0:T(8,128)} fusion(bf16[64,2,256]{2,1,0:T(2,128)(2,1)} %slice.3, s32[]{:T(128)S(6)} %select_n.7), kind=kLoop, calls=%fused_computation.4 | loop fusion | flops 128 | bytes 772 | tf_op jit(solution)/shard_map/reshape | solution.py:509
  63.4 0.9 reshape.31.source_ref
  64.3 0.0 collective-permute-done.before_ref
  64.3 0.0 collective-permute-done.1.after_ref
  64.3 0.0 copy-done.5
  64.3 0.0 copy-done.7
  64.3 0.0 copy-done.3
  64.3 0.0 copy-start.2
  64.3 2.3 %copy-done.2 = bf16[64,144,256]{2,1,0:T(8,128)(2,1)S(1)} copy-done((bf16[64,144,256]{2,1,0:T(8,128)(2,1)S(1)}, bf16[64,144,256]{2,1,0:T(8,128)(2,1)}, u32[]{:S(2)}) %copy-start.2) | copy-done | bytes 4718616
  66.6 0.0 copy-start.4
  66.6 1.2 copy-done.4
  67.9 5.6 %shard_map.104 = (bf16[512,256]{1,0:T(8,128)(2,1)}, bf16[256,256]{1,0:T(8,128)(2,1)S(1)}) custom-call(s32[128]{0:T(128)S(1)} %reshape.31.source_ref, s32[128]{0:T(128)S(1)} %reshape.28.dest_ref, s32[20]{0:T(128)S(1)} %reshape.29.position_ref, bf16[64,144,256]{2,1,0:T(8,128)(2,1)S(1)} %copy-done.2, bf16[64,64,128]{2,1,0:T(8,128)(2,1)S(1)} %bitcast.12, ...), custom_call_target="tpu_custom_call" | custom-call | tf_op jit(solution)/shard_map/pallas_call | solution.py:467
  73.4 0.0 copy-start.6
  73.4 0.7 copy-done.6
  74.1 31.4 %shard_map.105.gram_ref = bf16[4,256,256]{2,1,0:T(8,128)(2,1)} custom-call(bf16[256,256]{1,0:T(8,128)(2,1)} %copy-done.6), custom_call_target="tpu_custom_call" | custom-call | tf_op jit(solution)/shard_map/pallas_call | solution.py:364
  105.5 32.6 %shard_map.106 = (f32[256,256]{1,0:T(8,128)}, bf16[3,256,256]{2,1,0:T(8,128)(2,1)}) custom-call(bf16[4,256,256]{2,1,0:T(8,128)(2,1)} %shard_map.105.gram_ref), custom_call_target="tpu_custom_call" | custom-call | tf_op jit(solution)/shard_map/pallas_call | solution.py:80
  (1 shorter events, 0.0 us)
Async XLA Ops:
  0.6 13.4 %copy-start = (bf16[2,64,256]{2,1,0:T(8,128)(2,1)S(1)}, bf16[2,64,256]{2,1,0:T(8,128)(2,1)}, u32[]{:S(2)}) copy-start(bf16[2,64,256]{2,1,0:T(8,128)(2,1)} %param.12) | copy-start | bytes 196612
  0.6 63.6 %copy-start.5 = (bf16[512,256]{1,0:T(8,128)(2,1)S(1)}, bf16[512,256]{1,0:T(8,128)(2,1)}, u32[]{:S(2)}) copy-start(bf16[512,256]{1,0:T(8,128)(2,1)} %own_ref.1) | copy-start | bytes 786436
  0.7 63.6 %copy-start.7 = (bf16[2,64,256]{2,1,0:T(8,128)(2,1)S(1)}, bf16[2,64,256]{2,1,0:T(8,128)(2,1)}, u32[]{:S(2)}) copy-start(bf16[2,64,256]{2,1,0:T(8,128)(2,1)} %basis_ref.1) | copy-start | bytes 196612
  0.7 63.6 %copy-start.3 = (bf16[2,10,256,256]{3,2,1,0:T(8,128)(2,1)S(1)}, bf16[2,10,256,256]{3,2,1,0:T(8,128)(2,1)}, u32[]{:S(2)}) copy-start(bf16[2,10,256,256]{3,2,1,0:T(8,128)(2,1)} %block_ref.1) | copy-start | bytes 7864324
  0.7 63.6 %collective-permute-start = (bf16[512,256]{1,0:T(8,128)(2,1)}, bf16[512,256]{1,0:T(8,128)(2,1)S(1)}, u32[]{:S(2)}, u32[]{:S(2)}) collective-permute-start(bf16[512,256]{1,0:T(8,128)(2,1)} %own_ref.1), channel_id=1, source_target_pairs={{0,1},{1,2},{2,3},{3,4},{4,5},{5,6},{6,7},{7,8},{8,9},{9,10},{10,1... | collective-permute-start | bytes 786440 | tf_op jit(solution)/shard_map/ppermute | solution.py:484
  5.5 58.7 %collective-permute-start.1 = (bf16[512,256]{1,0:T(8,128)(2,1)}, bf16[512,256]{1,0:T(8,128)(2,1)S(1)}, u32[]{:S(2)}, u32[]{:S(2)}) collective-permute-start(bf16[512,256]{1,0:T(8,128)(2,1)} %own_ref.1), channel_id=1, source_target_pairs={{1,0},{2,1},{3,2},{4,3},{5,4},{6,5},{7,6},{8,7},{9,8},{10,9},{11,1... | collective-permute-start | bytes 786440 | tf_op jit(solution)/shard_map/ppermute | solution.py:484
  58.6 2.1 %copy-start.1 = (bf16[64,144,256]{2,1,0:T(8,128)(2,1)}, bf16[64,144,256]{2,1,0:T(8,128)(2,1)S(1)}, u32[]{:S(2)}) copy-start(bf16[64,144,256]{2,1,0:T(8,128)(2,1)S(1)} %shard_map.103.gathered_ref) | copy-start | bytes 14155780
  64.3 2.3 %copy-start.2 = (bf16[64,144,256]{2,1,0:T(8,128)(2,1)S(1)}, bf16[64,144,256]{2,1,0:T(8,128)(2,1)}, u32[]{:S(2)}) copy-start(bf16[64,144,256]{2,1,0:T(8,128)(2,1)} %copy-done.1) | copy-start | bytes 14155780
  66.6 1.2 copy-start.4
  73.4 0.7 copy-start.6

commit v4 on v3

--- a/solution.py
+++ b/solution.py
@@ -11,6 +11,7 @@
 
 BLOCK = 32
 GROUP = 8
+PIVOTS = 4
 
 
 def dot32(a, b, dims):
@@ -29,19 +30,42 @@
     for d in blocks:
         x = jnp.concatenate([d, eye], axis=1)
         states.append([x[g * GROUP : (g + 1) * GROUP] for g in range(size // GROUP)])
-    for k in range(size):
+    full = (GROUP, 2 * size)
+    for k in range(0, size, PIVOTS):
         own, r = divmod(k, GROUP)
         for x in states:
-            line = x[own][r : r + 1, :]
-            scale = lax.rsqrt(line[:, k : k + 1])
-            line = line * scale
+            lines = [jnp.broadcast_to(x[own][r + i : r + i + 1, :], full) for i in range(PIVOTS)]
+            held = {
+                (i, j): jnp.broadcast_to(x[own][r + i : r + i + 1, k + j : k + j + 1], full)
+                for i in range(PIVOTS)
+                for j in range(i, PIVOTS)
+            }
+            columns = [
+                [jnp.broadcast_to(x[g][:, k + j : k + j + 1], full) for j in range(PIVOTS)]
+                for g in range(own, size // GROUP)
+            ]
+            for i in range(PIVOTS):
+                scale = lax.rsqrt(held[i, i])
+                lines[i] = lines[i] * scale
+                for j in range(i + 1, PIVOTS):
+                    held[i, j] = held[i, j] * scale
+                for j in range(i + 1, PIVOTS):
+                    lines[j] = lines[j] - held[i, j] * lines[i]
+                    for m in range(j, PIVOTS):
+                        held[j, m] = held[j, m] - held[i, j] * held[i, m]
+                for column in columns:
+                    column[i] = column[i] * scale
+                    for j in range(i + 1, PIVOTS):
+                        column[j] = column[j] - column[i] * held[i, j]
             for g in range(own, size // GROUP):
-                factor = x[g][:, k : k + 1] * scale
+                below = x[g]
+                for i in range(PIVOTS):
+                    below = below - columns[g - own][i] * lines[i]
                 if g == own:
-                    below = x[g] - jnp.where(sub > r, factor, 0.0) * line
-                    x[g] = jnp.where(sub == r, line, below)
-                else:
-                    x[g] = x[g] - factor * line
+                    below = jnp.where(sub >= r + PIVOTS, below, x[g])
+                    for i in range(PIVOTS):
+                        below = jnp.where(sub == r + i, lines[i], below)
+                x[g] = below
     out = []
     for x in states:
         x = jnp.concatenate(x, axis=0)
@@ -386,8 +410,8 @@
     source_ref,
     dest_ref,
     position_ref,
-    gathered_ref,
-    coupling_ref,
+    gathered_hbm,
+    coupling_hbm,
     basis_ref,
     block_ref,
     before_ref,
@@ -396,6 +420,10 @@
     samples_ref,
     gram_ref,
     extended,
+    gathered_ref,
+    coupling_ref,
+    near_sum,
+    sems,
 ):
     leaf_count, rank, leaf_rows = basis_ref.shape
     seg_count = coupling_ref.shape[0]
@@ -403,8 +431,28 @@
     width = gathered_ref.shape[2]
     near_count = block_ref.shape[1]
     own_rows = own_ref.shape[0]
+    loads = [
+        pltpu.make_async_copy(gathered_hbm, gathered_ref, sems.at[0]),
+        pltpu.make_async_copy(coupling_hbm, coupling_ref, sems.at[1]),
+    ]
+    for load in loads:
+        load.start()
     for index, part in enumerate((before_ref, own_ref, after_ref)):
         extended[index * own_rows : (index + 1) * own_rows, :] = part[...]
+    for leaf in range(leaf_count):
+        picked = []
+        for entry in range(near_count):
+            position = position_ref[leaf, entry]
+            start = pl.multiple_of(jnp.maximum(position, 0) * leaf_rows, leaf_rows)
+            value = extended[pl.ds(start, leaf_rows), :]
+            picked.append(jnp.where(position >= 0, value, jnp.zeros_like(value)))
+        near_sum[leaf * leaf_rows : (leaf + 1) * leaf_rows, :] = jnp.dot(
+            jnp.concatenate([block_ref[leaf, entry] for entry in range(near_count)], axis=1),
+            jnp.concatenate(picked, axis=0),
+            preferred_element_type=jnp.float32,
+        )
+    for load in loads:
+        load.wait()
     lane = lax.broadcasted_iota(jnp.int32, (1, slots * rank), 1) // rank
 
     def step(index, total):
@@ -413,8 +461,8 @@
             seg = index * FAR_UNROLL + part
             key = jnp.full((1, slots * rank), -1, jnp.int32)
             for slot in range(slots):
-                source = source_ref[seg * slots + slot]
-                served = jnp.where(source < leaf_count, dest_ref[seg * slots + slot], -1)
+                source = source_ref[slot, seg]
+                served = jnp.where(source < leaf_count, dest_ref[slot, seg], -1)
                 key = jnp.where(lane == slot, served, key)
                 start = pl.multiple_of(jnp.minimum(source, leaf_count - 1) * rank, rank)
                 right.append(gathered_ref[seg, pl.ds(start, rank), :])
@@ -443,18 +491,7 @@
             (((0,), (0,)), ((), ())),
             preferred_element_type=jnp.float32,
         )
-        picked = []
-        for entry in range(near_count):
-            position = position_ref[leaf * near_count + entry]
-            start = pl.multiple_of(jnp.maximum(position, 0) * leaf_rows, leaf_rows)
-            value = extended[pl.ds(start, leaf_rows), :]
-            picked.append(jnp.where(position >= 0, value, jnp.zeros_like(value)))
-        near = jnp.dot(
-            jnp.concatenate([block_ref[leaf, entry] for entry in range(near_count)], axis=1),
-            jnp.concatenate(picked, axis=0),
-            preferred_element_type=jnp.float32,
-        )
-        samples_ref[rows, :] = (near + far).astype(jnp.bfloat16)
+        samples_ref[rows, :] = (near_sum[rows, :] + far).astype(jnp.bfloat16)
     samples = samples_ref[...]
     gram_ref[...] = lax.dot_general(
         samples, samples, (((0,), (0,)), ((), ())), preferred_element_type=jnp.float32
@@ -470,9 +507,15 @@
             jax.ShapeDtypeStruct((rows, width), jnp.bfloat16),
             jax.ShapeDtypeStruct((width, width), jnp.bfloat16),
         ),
-        in_specs=[smem] * 3 + [vmem] * 7,
+        in_specs=[smem] * 3 + [pl.BlockSpec(memory_space=pl.ANY)] * 2 + [vmem] * 5,
         out_specs=[vmem, vmem],
-        scratch_shapes=[pltpu.VMEM((3 * rows, width), own.dtype)],
+        scratch_shapes=[
+            pltpu.VMEM((3 * rows, width), own.dtype),
+            pltpu.VMEM(gathered.shape, gathered.dtype),
+            pltpu.VMEM(coupling.shape, coupling.dtype),
+            pltpu.VMEM((rows, width), jnp.float32),
+            pltpu.SemaphoreType.DMA((2,)),
+        ],
         compiler_params=pltpu.CompilerParams(vmem_limit_bytes=32 * 2**20),
     )(source, dest, position, gathered, coupling, basis, blocks, before, own, after)
 
@@ -506,14 +549,14 @@
     gathered = gather_segments(packed)
     sources = gathered[:, leaf_count * rank_width : leaf_count * rank_width + slot_number_count, :]
     sources = lax.dynamic_slice_in_dim(sources, lax.axis_index("seg"), 1, axis=2)
-    sources = sources.astype(jnp.int32).reshape(seg_count * slot_number_count)
+    sources = jnp.swapaxes(sources.astype(jnp.int32)[:, :, 0], 0, 1)
     before, after = neighbours(sample_cols, ("seg", "sub"))
     base_leaf = (lax.axis_index(("seg", "sub")) - 1) * leaf_count
     position = jnp.where(near_list >= 0, near_list - base_leaf, -1)
     samples, gram_local = far_and_gram(
         sources,
-        far_dest.reshape(seg_count * slot_number_count),
-        position.reshape(leaf_count * near_count),
+        jnp.swapaxes(far_dest[0, 0], 0, 1),
+        position,
         gathered,
         couplings[0, 0],
         row_basis_t,

time: 139 us -> 128 us (0.921)
  Pallas kernels: 112 us -> 106 us
  local copies, waits for them, and re-layouts: 10.3 us -> 7.95 us
  other arithmetic: 3.99 us -> 2.19 us
    pallas_call x1, Pallas kernels: 32.6 us -> 25.8 us  [factors(): pl.pallas_call(factor_kernel, out_shape=(jax.ShapeDtypeStruct((n, n), jnp...]
    reshape x1 -> x0, other arithmetic: 2.6 us -> none  [body(): sources = sources.astype(jnp.int32).reshape(seg_count * slot_number_count)]
    reshape x3 -> x0, local copies, waits for them, and re-layouts: 1.86 us -> none  [the longest x1 0.89 us: body(): far_dest.reshape(seg_count * slot_number_count)]
    transpose x0 -> x1, other arithmetic: none -> 1.49 us  [body(): sources = jnp.swapaxes(sources.astype(jnp.int32)[:, :, 0], 0, 1)]
    unnamed x17 -> x20, local copies, waits for them, and re-layouts: 7.74 us -> 6.36 us
  transfers between devices with their start and end apart: 2 -> 2, of which waited for: 0 -> 0; matrix products, arithmetic and copies ran while one was open for 7% -> 4% of each run, Pallas kernels for 30% -> 34%
where the time goes in v4:
time: 128 us
  Pallas kernels  106 us (83%)
  starting transfers between devices  10.3 us (8%)
  local copies, waits for them, and re-layouts  7.95 us (6%)
  other arithmetic  2.19 us (2%)
    pallas_call x1, Pallas kernels, gather_segments(): pl.pallas_call(gather_kernel, out_shape=jax.ShapeDtypeStruct((seg_count,...  43.2 us
    pallas_call x1, Pallas kernels, level_grams(): pl.pallas_call(functools.partial(gram_kernel, rows_each), out_shape=jax.S...  30.4 us
    pallas_call x1, Pallas kernels, factors(): pl.pallas_call(factor_kernel, out_shape=(jax.ShapeDtypeStruct((n, n), jnp...  25.8 us
    ppermute x2, starting transfers between devices, neighbours(): return (lax.ppermute(value, axes, up), lax.ppermute(value, axes, down))  10.3 us
    unnamed x20, local copies, waits for them, and re-layouts  6.36 us
    pallas_call x1, Pallas kernels, far_and_gram(): pl.pallas_call(far_kernel, out_shape=(jax.ShapeDtypeStruct((rows, width),...  6.2 us
  transfers between devices with their start and end apart: 2, of which 0 were waited for; matrix products, arithmetic and copies ran while one was open for 4% of the time, Pallas kernels for 34%

profile of v4, /device:TPU:1, one launch (start us, length us, event | category | flops | bytes accessed | tf_op | source)
XLA Modules:
  0.0 127.9 jit_solution(14348830660863444414)
XLA Ops:
  0.6 0.0 copy-start
  0.6 0.0 copy-start.4
  0.7 0.0 copy-start.9
  0.7 0.0 copy-start.8
  0.7 0.0 copy-start.7
  0.7 0.0 copy-start.3
  0.7 4.8 %collective-permute-start = (bf16[512,256]{1,0:T(8,128)(2,1)}, bf16[512,256]{1,0:T(8,128)(2,1)S(1)}, u32[]{:S(2)}, u32[]{:S(2)}) collective-permute-start(bf16[512,256]{1,0:T(8,128)(2,1)} %own_ref.1), channel_id=1, source_target_pairs={{0,1},{1,2},{2,3},{3,4},{4,5},{5,6},{6,7},{7,8},{8,9},{9,10},{10,1... | collective-permute-start | bytes 786440 | tf_op jit(solution)/shard_map/ppermute | solution.py:527
  5.6 5.5 %collective-permute-start.1 = (bf16[512,256]{1,0:T(8,128)(2,1)}, bf16[512,256]{1,0:T(8,128)(2,1)S(1)}, u32[]{:S(2)}, u32[]{:S(2)}) collective-permute-start(bf16[512,256]{1,0:T(8,128)(2,1)} %own_ref.1), channel_id=1, source_target_pairs={{1,0},{2,1},{3,2},{4,3},{5,4},{6,5},{7,6},{8,7},{9,8},{10,9},{11,1... | collective-permute-start | bytes 786440 | tf_op jit(solution)/shard_map/ppermute | solution.py:527
  11.0 0.7 convert_bitcast_fusion
  11.7 0.0 copy-done
  11.7 1.1 convolution_convert_fusion
  12.9 43.2 %shard_map.103.gathered_hbm = bf16[64,144,256]{2,1,0:T(8,128)(2,1)S(1)} custom-call(bf16[144,256]{1,0:T(8,128)(2,1)S(1)} %fusion.1.own_ref), custom_call_target="tpu_custom_call" | custom-call | tf_op jit(solution)/shard_map/pallas_call | solution.py:266
  56.0 0.7 slice.3
  56.7 0.0 copy-start.1
  56.7 2.1 %copy-done.1 = bf16[64,144,256]{2,1,0:T(8,128)(2,1)} copy-done((bf16[64,144,256]{2,1,0:T(8,128)(2,1)}, bf16[64,144,256]{2,1,0:T(8,128)(2,1)S(1)}, u32[]{:S(2)}) %copy-start.1) | copy-done | bytes 4718616
  58.8 1.5 %dynamic-slice_convert_fusion = s32[64,2,1]{2,1,0:T(2,128)} fusion(bf16[64,2,256]{2,1,0:T(2,128)(2,1)} %slice.3, s32[]{:T(128)S(6)} %select_n.7), kind=kLoop, calls=%fused_computation.4 | loop fusion | flops 128 | bytes 772 | tf_op jit(solution)/shard_map/transpose | solution.py:552
  60.3 0.9 copy.12
  61.2 0.0 copy-done.9
  61.3 0.0 collective-permute-done.before_ref
  61.3 0.0 collective-permute-done.1.after_ref
  61.3 0.0 copy-done.4
  61.3 0.0 copy-done.8
  61.3 0.0 copy-done.7
  61.3 0.0 copy-done.3
  61.3 0.0 copy-start.2
  61.3 2.3 %copy-done.2 = bf16[64,144,256]{2,1,0:T(8,128)(2,1)S(1)} copy-done((bf16[64,144,256]{2,1,0:T(8,128)(2,1)S(1)}, bf16[64,144,256]{2,1,0:T(8,128)(2,1)}, u32[]{:S(2)}) %copy-start.2) | copy-done | bytes 4718616
  63.7 0.0 copy-start.5
  63.7 1.2 copy-done.5
  64.9 6.2 %shard_map.104 = (bf16[512,256]{1,0:T(8,128)(2,1)}, bf16[256,256]{1,0:T(8,128)(2,1)S(1)}) custom-call(s32[2,64]{1,0:T(2,128)S(1)} %bitcast.18, s32[2,64]{1,0:T(2,128)S(1)} %bitcast.19, s32[2,10]{1,0:T(2,128)S(1)} %compare_select_fusion.position_ref, bf16[64,144,256]{2,1,0:T(8,128)(2,1)S(1)} %copy-done.2, bf16[64,64,128]{2,1,0:T(8,128)(2,1)S(1)} %bitcast.17, ...), custom_call_target="tpu_custom_call" | custom-call | tf_op jit(solution)/shard_map/pallas_call | solution.py:504
  71.1 0.0 copy-start.6
  71.1 0.6 copy-done.6
  71.7 30.4 %shard_map.105.gram_ref = bf16[4,256,256]{2,1,0:T(8,128)(2,1)} custom-call(bf16[256,256]{1,0:T(8,128)(2,1)} %copy-done.6), custom_call_target="tpu_custom_call" | custom-call | tf_op jit(solution)/shard_map/pallas_call | solution.py:388
  102.1 25.8 %shard_map.106 = (f32[256,256]{1,0:T(8,128)}, bf16[3,256,256]{2,1,0:T(8,128)(2,1)}) custom-call(bf16[4,256,256]{2,1,0:T(8,128)(2,1)} %shard_map.105.gram_ref), custom_call_target="tpu_custom_call" | custom-call | tf_op jit(solution)/shard_map/pallas_call | solution.py:104
  (2 shorter events, 0.0 us)
Async XLA Ops:
  0.6 11.1 %copy-start = (bf16[2,64,256]{2,1,0:T(8,128)(2,1)S(1)}, bf16[2,64,256]{2,1,0:T(8,128)(2,1)}, u32[]{:S(2)}) copy-start(bf16[2,64,256]{2,1,0:T(8,128)(2,1)} %param.12) | copy-start | bytes 196612
  0.6 60.6 %copy-start.4 = (bf16[512,256]{1,0:T(8,128)(2,1)S(1)}, bf16[512,256]{1,0:T(8,128)(2,1)}, u32[]{:S(2)}) copy-start(bf16[512,256]{1,0:T(8,128)(2,1)} %own_ref.1) | copy-start | bytes 786436
  0.7 60.6 %copy-start.9 = (s32[2,10]{1,0:T(2,128)S(1)}, s32[2,10]{1,0:T(2,128)}, u32[]{:S(2)}) copy-start(s32[2,10]{1,0:T(2,128)} %param.10) | copy-start | bytes 244
  0.7 60.6 %copy-start.8 = (s32[1,1,64,2]{2,3,1,0:T(2,128)S(1)}, s32[1,1,64,2]{2,3,1,0:T(2,128)}, u32[]{:S(2)}) copy-start(s32[1,1,64,2]{2,3,1,0:T(2,128)} %param.15) | copy-start | bytes 1540
  0.7 60.6 %copy-start.7 = (bf16[2,64,256]{2,1,0:T(8,128)(2,1)S(1)}, bf16[2,64,256]{2,1,0:T(8,128)(2,1)}, u32[]{:S(2)}) copy-start(bf16[2,64,256]{2,1,0:T(8,128)(2,1)} %basis_ref.1) | copy-start | bytes 196612
  0.7 60.6 %copy-start.3 = (bf16[2,10,256,256]{3,2,1,0:T(8,128)(2,1)S(1)}, bf16[2,10,256,256]{3,2,1,0:T(8,128)(2,1)}, u32[]{:S(2)}) copy-start(bf16[2,10,256,256]{3,2,1,0:T(8,128)(2,1)} %block_ref.1) | copy-start | bytes 7864324
  0.7 60.6 %collective-permute-start = (bf16[512,256]{1,0:T(8,128)(2,1)}, bf16[512,256]{1,0:T(8,128)(2,1)S(1)}, u32[]{:S(2)}, u32[]{:S(2)}) collective-permute-start(bf16[512,256]{1,0:T(8,128)(2,1)} %own_ref.1), channel_id=1, source_target_pairs={{0,1},{1,2},{2,3},{3,4},{4,5},{5,6},{6,7},{7,8},{8,9},{9,10},{10,1... | collective-permute-start | bytes 786440 | tf_op jit(solution)/shard_map/ppermute | solution.py:527
  5.6 55.7 %collective-permute-start.1 = (bf16[512,256]{1,0:T(8,128)(2,1)}, bf16[512,256]{1,0:T(8,128)(2,1)S(1)}, u32[]{:S(2)}, u32[]{:S(2)}) collective-permute-start(bf16[512,256]{1,0:T(8,128)(2,1)} %own_ref.1), channel_id=1, source_target_pairs={{1,0},{2,1},{3,2},{4,3},{5,4},{6,5},{7,6},{8,7},{9,8},{10,9},{11,1... | collective-permute-start | bytes 786440 | tf_op jit(solution)/shard_map/ppermute | solution.py:527
  56.7 2.1 %copy-start.1 = (bf16[64,144,256]{2,1,0:T(8,128)(2,1)}, bf16[64,144,256]{2,1,0:T(8,128)(2,1)S(1)}, u32[]{:S(2)}) copy-start(bf16[64,144,256]{2,1,0:T(8,128)(2,1)S(1)} %shard_map.103.gathered_hbm) | copy-start | bytes 14155780
  61.3 2.3 %copy-start.2 = (bf16[64,144,256]{2,1,0:T(8,128)(2,1)S(1)}, bf16[64,144,256]{2,1,0:T(8,128)(2,1)}, u32[]{:S(2)}) copy-start(bf16[64,144,256]{2,1,0:T(8,128)(2,1)} %copy-done.1) | copy-start | bytes 14155780
  63.7 1.2 copy-start.5
  71.1 0.7 copy-start.6

commit v5 on v4

--- a/solution.py
+++ b/solution.py
@@ -267,7 +267,7 @@
         gather_kernel,
         out_shape=jax.ShapeDtypeStruct((seg_count, rows, width), value.dtype),
         in_specs=[pl.BlockSpec(memory_space=pltpu.VMEM)],
-        out_specs=pl.BlockSpec(memory_space=pltpu.VMEM),
+        out_specs=pl.BlockSpec(memory_space=pl.ANY),
         scratch_shapes=[
             dma,
             dma((3, 2)),
@@ -276,7 +276,7 @@
             dma((half + 1, 2, 2)),
         ],
         compiler_params=pltpu.CompilerParams(
-            collective_id=0, has_side_effects=True, vmem_limit_bytes=32 * 2**20
+            collective_id=0, has_side_effects=True, vmem_limit_bytes=56 * 2**20
         ),
     )(value)
 
@@ -516,7 +516,7 @@
             pltpu.VMEM((rows, width), jnp.float32),
             pltpu.SemaphoreType.DMA((2,)),
         ],
-        compiler_params=pltpu.CompilerParams(vmem_limit_bytes=32 * 2**20),
+        compiler_params=pltpu.CompilerParams(vmem_limit_bytes=56 * 2**20),
     )(source, dest, position, gathered, coupling, basis, blocks, before, own, after)
 
 

time: 128 us -> 129 us (level)
  Pallas kernels: 106 us -> 112 us
  local copies, waits for them, and re-layouts: 7.95 us -> 2.41 us
    unnamed x20 -> x8, local copies, waits for them, and re-layouts: 6.36 us -> 0.79 us
    pallas_call x1, Pallas kernels: 6.2 us -> 9.74 us  [far_and_gram(): pl.pallas_call(far_kernel, out_shape=(jax.ShapeDtypeStruct((rows, width),...]
    pallas_call x1, Pallas kernels: 43.2 us -> 45.3 us  [gather_segments(): pl.pallas_call(gather_kernel, out_shape=jax.ShapeDtypeStruct((seg_count,...]
    transpose x1, other arithmetic: 1.49 us -> 0.11 us  [body(): sources = jnp.swapaxes(sources.astype(jnp.int32)[:, :, 0], 0, 1)]
  transfers between devices with their start and end apart: 2 -> 2, of which waited for: 0 -> 0; matrix products, arithmetic and copies ran while one was open for 4% -> 4% of each run, Pallas kernels for 34% -> 35%
where the time goes in v5:
time: 129 us
  Pallas kernels  112 us (87%)
  starting transfers between devices  10.2 us (8%)
  local copies, waits for them, and re-layouts  2.41 us (2%)
  other arithmetic  2.01 us (2%)
    pallas_call x1, Pallas kernels, gather_segments(): pl.pallas_call(gather_kernel, out_shape=jax.ShapeDtypeStruct((seg_count,...  45.3 us
    pallas_call x1, Pallas kernels, level_grams(): pl.pallas_call(functools.partial(gram_kernel, rows_each), out_shape=jax.S...  31.2 us
    pallas_call x1, Pallas kernels, factors(): pl.pallas_call(factor_kernel, out_shape=(jax.ShapeDtypeStruct((n, n), jnp...  25.8 us
    ppermute x2, starting transfers between devices, neighbours(): return (lax.ppermute(value, axes, up), lax.ppermute(value, axes, down))  10.2 us
    pallas_call x1, Pallas kernels, far_and_gram(): pl.pallas_call(far_kernel, out_shape=(jax.ShapeDtypeStruct((rows, width),...  9.74 us
  transfers between devices with their start and end apart: 2, of which 0 were waited for; matrix products, arithmetic and copies ran while one was open for 4% of the time, Pallas kernels for 35%

profile of v5, /device:TPU:1, one launch (start us, length us, event | category | flops | bytes accessed | tf_op | source)
XLA Modules:
  0.0 128.6 jit_solution(11707599580307926359)
XLA Ops:
  0.6 0.0 copy-start
  0.6 0.0 copy-start.3
  0.7 4.7 %collective-permute-start = (bf16[512,256]{1,0:T(8,128)(2,1)}, bf16[512,256]{1,0:T(8,128)(2,1)S(1)}, u32[]{:S(2)}, u32[]{:S(2)}) collective-permute-start(bf16[512,256]{1,0:T(8,128)(2,1)} %own_ref.1), channel_id=1, source_target_pairs={{0,1},{1,2},{2,3},{3,4},{4,5},{5,6},{6,7},{7,8},{8,9},{9,10},{10,1... | collective-permute-start | bytes 786440 | tf_op jit(solution)/shard_map/ppermute | solution.py:527
  5.4 5.5 %collective-permute-start.1 = (bf16[512,256]{1,0:T(8,128)(2,1)}, bf16[512,256]{1,0:T(8,128)(2,1)S(1)}, u32[]{:S(2)}, u32[]{:S(2)}) collective-permute-start(bf16[512,256]{1,0:T(8,128)(2,1)} %own_ref.1), channel_id=1, source_target_pairs={{1,0},{2,1},{3,2},{4,3},{5,4},{6,5},{7,6},{8,7},{9,8},{10,9},{11,1... | collective-permute-start | bytes 786440 | tf_op jit(solution)/shard_map/ppermute | solution.py:527
  10.9 0.7 convert_bitcast_fusion
  11.5 0.0 copy-done
  11.6 1.1 convolution_convert_fusion
  12.7 0.6 fusion.1.own_ref
  13.3 45.3 %shard_map.103.gathered_hbm = bf16[64,144,256]{2,1,0:T(8,128)(2,1)} custom-call(bf16[144,256]{1,0:T(8,128)(2,1)} %fusion.1.own_ref), custom_call_target="tpu_custom_call" | custom-call | tf_op jit(solution)/shard_map/pallas_call | solution.py:266
  58.7 1.0 slice.3
  59.6 0.1 dynamic-slice_convert_fusion
  59.8 0.6 copy.12
  60.4 0.0 copy-done.3
  60.4 0.6 compare_select_fusion.position_ref
  61.0 0.0 collective-permute-done.before_ref
  61.0 0.0 copy-start.1
  61.0 0.0 collective-permute-done.1.after_ref
  61.0 0.0 copy-start.2
  61.0 0.7 copy-done.1
  61.7 0.1 copy-done.2
  61.8 9.7 %shard_map.104 = (bf16[512,256]{1,0:T(8,128)(2,1)}, bf16[256,256]{1,0:T(8,128)(2,1)}) custom-call(s32[2,64]{1,0:T(2,128)} %bitcast.19, s32[2,64]{1,0:T(2,128)} %bitcast.20, s32[2,10]{1,0:T(2,128)} %compare_select_fusion.position_ref, bf16[64,144,256]{2,1,0:T(8,128)(2,1)} %shard_map.103.gathered_hbm, bf16[64,64,128]{2,1,0:T(8,128)(2,1)} %bitcast.17, ...), custom_call_target="tpu_custom_call" | custom-call | tf_op jit(solution)/shard_map/pallas_call | solution.py:504
  71.5 31.2 %shard_map.105.gram_ref = bf16[4,256,256]{2,1,0:T(8,128)(2,1)} custom-call(bf16[256,256]{1,0:T(8,128)(2,1)} %get-tuple-element.8.local_ref), custom_call_target="tpu_custom_call" | custom-call | tf_op jit(solution)/shard_map/pallas_call | solution.py:388
  102.7 25.8 %shard_map.106 = (f32[256,256]{1,0:T(8,128)}, bf16[3,256,256]{2,1,0:T(8,128)(2,1)}) custom-call(bf16[4,256,256]{2,1,0:T(8,128)(2,1)} %shard_map.105.gram_ref), custom_call_target="tpu_custom_call" | custom-call | tf_op jit(solution)/shard_map/pallas_call | solution.py:104
Async XLA Ops:
  0.6 10.9 %copy-start = (bf16[2,64,256]{2,1,0:T(8,128)(2,1)S(1)}, bf16[2,64,256]{2,1,0:T(8,128)(2,1)}, u32[]{:S(2)}) copy-start(bf16[2,64,256]{2,1,0:T(8,128)(2,1)} %param.12) | copy-start | bytes 196612
  0.6 59.8 %copy-start.3 = (s32[2,10]{1,0:T(2,128)S(1)}, s32[2,10]{1,0:T(2,128)}, u32[]{:S(2)}) copy-start(s32[2,10]{1,0:T(2,128)} %param.10) | copy-start | bytes 244
  0.7 60.3 %collective-permute-start = (bf16[512,256]{1,0:T(8,128)(2,1)}, bf16[512,256]{1,0:T(8,128)(2,1)S(1)}, u32[]{:S(2)}, u32[]{:S(2)}) collective-permute-start(bf16[512,256]{1,0:T(8,128)(2,1)} %own_ref.1), channel_id=1, source_target_pairs={{0,1},{1,2},{2,3},{3,4},{4,5},{5,6},{6,7},{7,8},{8,9},{9,10},{10,1... | collective-permute-start | bytes 786440 | tf_op jit(solution)/shard_map/ppermute | solution.py:527
  5.4 55.6 %collective-permute-start.1 = (bf16[512,256]{1,0:T(8,128)(2,1)}, bf16[512,256]{1,0:T(8,128)(2,1)S(1)}, u32[]{:S(2)}, u32[]{:S(2)}) collective-permute-start(bf16[512,256]{1,0:T(8,128)(2,1)} %own_ref.1), channel_id=1, source_target_pairs={{1,0},{2,1},{3,2},{4,3},{5,4},{6,5},{7,6},{8,7},{9,8},{10,9},{11,1... | collective-permute-start | bytes 786440 | tf_op jit(solution)/shard_map/ppermute | solution.py:527
  61.0 0.7 copy-start.1
  61.0 0.8 copy-start.2
